TPU v7x, 32 devices: a whole 2x2x4 slice. The times are simulated.
32 devices in a mesh: section: 2 (over y), dp: 4 (over x, core), tensor: 4 (over z).
Axes of the slice: x: 2, y: 2, z: 4, core: 2. Of those that a mesh axis runs over, the one named last changes fastest.
Arguments:
- acts_in: bfloat16 [4, 1024, 4, 1024], P(None, 'tensor', 'dp'), may hold values from -6 to 6
- cotangent: bfloat16 [4, 1024, 4, 1024], P(None, 'tensor', 'dp'), may hold values from -6 to 6
- norm_gains: float32 [2, 2, 1024], P('section', None, ('dp', 'tensor')), may hold values from 0.5 to 1.5
- vec_bias: float32 [2, 4, 1024], P('section', None, ('dp', 'tensor')), may hold values from -1.8 to 1.8
- w_qkv: bfloat16 [2, 1024, 3072], P('section', 'dp', 'tensor'), may hold values from -0.25 to 0.25
- b_qkv: bfloat16 [2, 16, 192], P('section', 'tensor', 'dp'), may hold values from -1.796875 to 1.796875
- w_out: bfloat16 [2, 1024, 1024], P('section', 'tensor', 'dp'), may hold values from -0.75 to 0.75
- w_up: bfloat16 [2, 1024, 4096], P('section', 'dp', 'tensor'), may hold values from -0.1875 to 0.1875
- b_up: bfloat16 [2, 32, 128], P('section', 'tensor', 'dp'), may hold values from -1.796875 to 1.796875
- w_down: bfloat16 [2, 4096, 1024], P('section', 'tensor', 'dp'), may hold values from -0.09375 to 0.09375
Outputs:
- acts_out: bfloat16 [2, 4, 1024, 4, 1024], P('section', None, 'tensor', 'dp')
- grad_in: bfloat16 [2, 4, 1024, 4, 1024], P('section', None, 'tensor', 'dp')
- grad_norm_gains: float32 [2, 2, 1024], P('section', None, ('dp', 'tensor'))
- grad_vec_bias: float32 [2, 4, 1024], P('section', None, ('dp', 'tensor'))
- grad_w_qkv: float32 [2, 1024, 3072], P('section', 'dp', 'tensor')
- grad_b_qkv: float32 [2, 16, 192], P('section', 'tensor', 'dp')
- grad_w_out: float32 [2, 1024, 1024], P('section', 'tensor', 'dp')
- grad_w_up: float32 [2, 1024, 4096], P('section', 'dp', 'tensor')
- grad_b_up: float32 [2, 32, 128], P('section', 'tensor', 'dp')
- grad_w_down: float32 [2, 4096, 1024], P('section', 'tensor', 'dp')
All inputs are finite; a program needn't handle non-finite values.
Results may differ from a plain program's by a relative error of at most 0.025.
Values may be sent and summed in bfloat16 or wider, within the bound.
No kernel may reach another device: no remote copies, remote signals or barrier semaphores. Data moves between devices by JAX's collectives and lax.ppermute only.
A program may use at most 384 MiB of HBM per device.

v0:
```python
from functools import partial
import math

import jax
import jax.numpy as jnp
from jax import lax
from jax.sharding import PartitionSpec as P

ROT = 16
QBLOCK = 512
MICRO = 4


NORM_EPS = 1e-05
ROPE_BASE = 10000.0
MASK_FILL = -1e30


def from_behind(value, axis, by):
    length = lax.axis_size(axis)
    pairs = [(i, i + by) for i in range(length) if 0 <= i + by < length]
    return lax.ppermute(value, axis, pairs)


def layer_norm(values, norm_gain, norm_shift):
    average = jnp.mean(values, axis=-1, keepdims=True)
    centred = values - average
    variance = jnp.mean(centred * centred, axis=-1, keepdims=True)
    return centred * lax.rsqrt(variance + NORM_EPS) * norm_gain + norm_shift


def both_norms(values, gain_attn, shift_attn, gain_mlp, shift_mlp):
    return (layer_norm(values, gain_attn, shift_attn), layer_norm(values, gain_mlp, shift_mlp))


def rotary_tables(length):
    half_rot = ROT // 2
    frequency = jnp.exp(
        jnp.arange(half_rot, dtype=jnp.float32) * (-2.0 * math.log(ROPE_BASE) / ROT)
    )
    angles = jnp.arange(length, dtype=jnp.float32)[:, None] * frequency[None, :]
    return (jnp.cos(angles), jnp.sin(angles))


def rotate(values, cosine, sine_tab):
    half_rot = ROT // 2
    low_half = values[..., :half_rot]
    high_half = values[..., half_rot:ROT]
    return jnp.concatenate(
        [
            low_half * cosine - high_half * sine_tab,
            high_half * cosine + low_half * sine_tab,
            values[..., ROT:],
        ],
        axis=-1,
    )


def rotate_back(grads_rot, cosine, sine_tab):
    half_rot = ROT // 2
    low_half = grads_rot[..., :half_rot]
    high_half = grads_rot[..., half_rot:ROT]
    return jnp.concatenate(
        [
            low_half * cosine + high_half * sine_tab,
            high_half * cosine - low_half * sine_tab,
            grads_rot[..., ROT:],
        ],
        axis=-1,
    )


def causal_scores(queries, key_rows, first_row, score_scale):
    block_rows = queries.shape[0]
    last_row = key_rows.shape[0]
    scores = (
        jnp.einsum("qshd,kshd->shqk", queries, key_rows, preferred_element_type=jnp.float32)
        * score_scale
    )
    row_pos = first_row + jnp.arange(block_rows, dtype=jnp.int32)
    col_pos = jnp.arange(last_row, dtype=jnp.int32)
    allowed = col_pos[None, :] <= row_pos[:, None]
    return (scores, allowed)


def attend(queries, key_rows, val_rows):
    length = queries.shape[0]
    block_rows = min(QBLOCK, length)
    score_scale = queries.shape[-1] ** (-0.5)
    outputs = []
    totals = []
    for block_index in range(length // block_rows):
        first_row = block_index * block_rows
        last_row = first_row + block_rows
        scores, allowed = causal_scores(
            queries[first_row:last_row], key_rows[:last_row], first_row, score_scale
        )
        scores = jnp.where(allowed, scores, MASK_FILL)
        highest = jnp.max(scores, axis=-1, keepdims=True)
        exponent = jnp.exp(scores - highest)
        denominator = jnp.sum(exponent, axis=-1, keepdims=True)
        probability = (exponent / denominator).astype(jnp.bfloat16)
        block_out = jnp.einsum(
            "shqk,kshd->qshd", probability, val_rows[:last_row], preferred_element_type=jnp.float32
        )
        outputs.append(block_out.astype(jnp.bfloat16))
        totals.append((highest + jnp.log(denominator))[..., 0])
    context = jnp.concatenate(outputs, axis=0)
    return (context.reshape(length, context.shape[1], -1), jnp.concatenate(totals, axis=-1))


def attend_back(queries, key_rows, val_rows, d_context, log_total):
    length = queries.shape[0]
    block_rows = min(QBLOCK, length)
    score_scale = queries.shape[-1] ** (-0.5)
    grad_query_list = []
    grad_keys = jnp.zeros(queries.shape, jnp.float32)
    grad_vals = jnp.zeros(queries.shape, jnp.float32)
    for block_index in range(length // block_rows):
        first_row = block_index * block_rows
        last_row = first_row + block_rows
        query_block = queries[first_row:last_row]
        scores, allowed = causal_scores(query_block, key_rows[:last_row], first_row, score_scale)
        probability = jnp.where(
            allowed, jnp.exp(scores - log_total[:, :, first_row:last_row, None]), 0.0
        )
        d_block = d_context[first_row:last_row]
        d_prob = jnp.einsum(
            "qshd,kshd->shqk", d_block, val_rows[:last_row], preferred_element_type=jnp.float32
        )
        delta = jnp.sum(probability * d_prob, axis=-1, keepdims=True)
        d_scores = (probability * (d_prob - delta)).astype(jnp.bfloat16)
        grad_query_list.append(
            jnp.einsum(
                "shqk,kshd->qshd", d_scores, key_rows[:last_row], preferred_element_type=jnp.float32
            )
            * score_scale
        )
        grad_keys = grad_keys.at[:last_row].add(
            jnp.einsum("shqk,qshd->kshd", d_scores, query_block, preferred_element_type=jnp.float32)
            * score_scale
        )
        grad_vals = grad_vals.at[:last_row].add(
            jnp.einsum(
                "shqk,qshd->kshd",
                probability.astype(jnp.bfloat16),
                d_block,
                preferred_element_type=jnp.float32,
            )
        )
    return (jnp.concatenate(grad_query_list, axis=0), grad_keys, grad_vals)


def local(acts_in, cotangent, norm_gains, vec_bias, w_qkv, b_qkv, w_out, w_up, b_up, w_down):
    section_index = lax.axis_index("section")
    own_start = lax.axis_index("tensor") * acts_in.shape[1]
    local_len = acts_in.shape[1]
    seq_count = acts_in.shape[2]
    model_width = acts_in.shape[3]
    length = local_len * lax.axis_size("tensor")
    all_rows = length * seq_count
    gain_full, bias_full = (
        lax.all_gather(norm_gains[0], ("dp", "tensor"), axis=1, tiled=True),
        lax.all_gather(vec_bias[0], ("dp", "tensor"), axis=1, tiled=True),
    )
    mat_qkv, bias_qkv, mat_out, mat_up, bias_up, mat_down = (
        lax.all_gather(w_qkv[0], "dp", axis=0, tiled=True),
        lax.all_gather(b_qkv[0], "dp", axis=1, tiled=True),
        lax.all_gather(w_out[0], "dp", axis=1, tiled=True),
        lax.all_gather(w_up[0], "dp", axis=0, tiled=True),
        lax.all_gather(b_up[0], "dp", axis=1, tiled=True),
        lax.all_gather(w_down[0], "dp", axis=1, tiled=True),
    )
    head_count = bias_qkv.shape[0]
    head_dim = bias_qkv.shape[1] // 3
    qkv_shift = bias_qkv.reshape(-1).astype(jnp.float32)
    up_shift = bias_up.reshape(-1).astype(jnp.float32)
    cosine, sine_tab = rotary_tables(length)
    cosine = cosine[:, None, None, :]
    sine_tab = sine_tab[:, None, None, :]
    received = jnp.zeros_like(acts_in[0])
    stash_list = []
    out_list = []
    for moment in range(MICRO + 1):
        own_rows = acts_in[min(moment, MICRO - 1)]
        inputs = jnp.where(section_index == 0, own_rows, received)
        forward_gathered = lax.all_gather(inputs, "tensor", axis=0, tiled=True)
        full_attn, full_mlp = both_norms(
            forward_gathered.astype(jnp.float32),
            gain_full[0],
            bias_full[0],
            gain_full[1],
            bias_full[1],
        )
        forward_normed_attn = full_attn.astype(jnp.bfloat16)
        forward_normed_mlp = full_mlp.astype(jnp.bfloat16)
        forward_flat_attn = forward_normed_attn.reshape(all_rows, model_width)
        forward_flat_mlp = forward_normed_mlp.reshape(all_rows, model_width)
        projected = (
            jnp.dot(forward_flat_attn, mat_qkv, preferred_element_type=jnp.float32) + qkv_shift
        )
        projected = projected.reshape(length, seq_count, head_count, 3, head_dim)
        forward_queries = rotate(projected[:, :, :, 0], cosine, sine_tab).astype(jnp.bfloat16)
        forward_key_rows = rotate(projected[:, :, :, 1], cosine, sine_tab).astype(jnp.bfloat16)
        forward_val_rows = projected[:, :, :, 2].astype(jnp.bfloat16)
        forward_context, forward_log_total = attend(
            forward_queries, forward_key_rows, forward_val_rows
        )
        forward_up_proj = (
            jnp.dot(forward_flat_mlp, mat_up, preferred_element_type=jnp.float32) + up_shift
        )
        forward_activated = jax.nn.gelu(forward_up_proj, approximate=False).astype(jnp.bfloat16)
        active_rows = forward_activated.reshape(length, seq_count, -1)
        context_part = forward_context.reshape(lax.axis_size("tensor") * local_len * seq_count, -1)
        active_part = active_rows.reshape(lax.axis_size("tensor") * local_len * seq_count, -1)
        summed = jnp.dot(context_part, mat_out, preferred_element_type=jnp.float32) + jnp.dot(
            active_part, mat_down, preferred_element_type=jnp.float32
        )
        mixed_sum = lax.psum_scatter(
            summed.reshape(lax.axis_size("tensor") * local_len, seq_count, model_width),
            "tensor",
            scatter_dimension=0,
            tiled=True,
        )
        result = inputs.astype(jnp.float32) + mixed_sum + bias_full[2] + bias_full[3]
        forward_stashed = (
            forward_gathered,
            forward_normed_attn,
            forward_normed_mlp,
            forward_queries,
            forward_key_rows,
            forward_val_rows,
            forward_context,
            forward_log_total,
            forward_up_proj,
            forward_activated,
        )
        result, stashed = (result.astype(jnp.bfloat16), forward_stashed)
        stash_list.append(stashed)
        out_list.append(result)
        if moment < MICRO:
            received = from_behind(result, "section", 1)
    stash_all = jax.tree.map(lambda *parts: jnp.stack(parts), *stash_list)
    acts_local = lax.dynamic_slice_in_dim(jnp.stack(out_list), section_index, MICRO, 0)
    back_received = jnp.zeros_like(cotangent[0])
    grad_list = []
    weight_sums = None
    vector_sums = None
    for moment in range(MICRO + 1):
        micro_index = moment - 1 + section_index
        is_valid = (micro_index >= 0) & (micro_index < MICRO)
        source_clock = jnp.clip(micro_index + section_index, 0, MICRO)
        stashed = jax.tree.map(
            lambda part: lax.dynamic_index_in_dim(part, source_clock, 0, keepdims=False), stash_all
        )
        upstream = jnp.where(section_index == 1, cotangent[min(moment, MICRO - 1)], back_received)
        (
            gathered,
            normed_attn,
            normed_mlp,
            queries,
            key_rows,
            val_rows,
            context,
            log_total,
            up_proj,
            activated,
        ) = stashed
        backward_inputs = lax.dynamic_slice_in_dim(gathered, own_start, local_len, 0)
        upstream_rows = lax.all_gather(upstream, "tensor", axis=0, tiled=True)
        flat_grad = upstream_rows.reshape(all_rows, model_width)
        d_context = jnp.dot(flat_grad, mat_out.T, preferred_element_type=jnp.float32).astype(
            jnp.bfloat16
        )
        d_context = d_context.reshape(length, seq_count, head_count, head_dim)
        d_active = jnp.dot(flat_grad, mat_down.T, preferred_element_type=jnp.float32)
        _, gelu_pullback = jax.vjp(partial(jax.nn.gelu, approximate=False), up_proj)
        d_up = gelu_pullback(d_active)[0].astype(jnp.bfloat16)
        grad_query, grad_key, grad_val = attend_back(
            queries, key_rows, val_rows, d_context, log_total
        )
        d_qkv = jnp.stack(
            [
                rotate_back(grad_query, cosine, sine_tab),
                rotate_back(grad_key, cosine, sine_tab),
                grad_val,
            ],
            axis=3,
        ).astype(jnp.bfloat16)
        d_qkv_flat = d_qkv.reshape(all_rows, -1)
        d_qkv_rows = d_qkv.reshape(length, seq_count, -1)
        d_up_rows = d_up.reshape(length, seq_count, -1)
        flat_attn = normed_attn.reshape(all_rows, model_width)
        flat_mlp = normed_mlp.reshape(all_rows, model_width)
        weight_terms = (
            jnp.einsum("tc,te->ce", flat_attn, d_qkv_flat, preferred_element_type=jnp.float32),
            jnp.sum(d_qkv_flat.astype(jnp.float32), axis=0).reshape(bias_qkv.shape),
            jnp.einsum(
                "tc,te->ce",
                context.reshape(all_rows, -1),
                flat_grad,
                preferred_element_type=jnp.float32,
            ),
            jnp.einsum("tc,te->ce", flat_mlp, d_up, preferred_element_type=jnp.float32),
            jnp.sum(d_up.astype(jnp.float32), axis=0).reshape(bias_up.shape),
            jnp.einsum("tc,te->ce", activated, flat_grad, preferred_element_type=jnp.float32),
        )
        attn_part = d_qkv_rows.reshape(lax.axis_size("tensor") * local_len * seq_count, -1)
        mlp_part = d_up_rows.reshape(lax.axis_size("tensor") * local_len * seq_count, -1)
        joined = jnp.concatenate(
            [
                jnp.dot(attn_part, mat_qkv.T, preferred_element_type=jnp.float32),
                jnp.dot(mlp_part, mat_up.T, preferred_element_type=jnp.float32),
            ],
            axis=-1,
        )
        d_normed = lax.psum_scatter(
            joined.reshape(lax.axis_size("tensor") * local_len, seq_count, 2 * model_width).astype(
                jnp.bfloat16
            ),
            "tensor",
            scatter_dimension=0,
            tiled=True,
        ).astype(jnp.float32)
        _, norm_pullback = jax.vjp(
            both_norms,
            backward_inputs.astype(jnp.float32),
            gain_full[0],
            bias_full[0],
            gain_full[1],
            bias_full[1],
        )
        d_local, d_gain_attn, d_shift_attn, d_gain_mlp, d_shift_mlp = norm_pullback(
            (d_normed[..., :model_width], d_normed[..., model_width:])
        )
        upstream_float = upstream.astype(jnp.float32)
        d_inputs = (upstream_float + d_local).astype(jnp.bfloat16)
        out_shift = jnp.sum(upstream_float, axis=(0, 1))
        vector_terms = (
            jnp.stack([d_gain_attn, d_gain_mlp]),
            jnp.stack([d_shift_attn, d_shift_mlp, out_shift, out_shift]),
        )
        d_inputs, weight_terms, vector_terms = (d_inputs, weight_terms, vector_terms)
        grad_list.append(d_inputs)
        if moment < MICRO:
            back_received = from_behind(d_inputs, "section", -1)
        weight_terms = tuple((jnp.where(is_valid, term, 0.0) for term in weight_terms))
        vector_terms = tuple((jnp.where(is_valid, term, 0.0) for term in vector_terms))
        if moment == 0:
            weight_sums = tuple(weight_terms)
            vector_sums = vector_terms
        else:
            weight_sums = tuple((a + b for a, b in zip(weight_sums, weight_terms)))
            vector_sums = tuple((a + b for a, b in zip(vector_sums, vector_terms)))
    sum_qkv, sum_bqkv, sum_out, sum_up, sum_bup, sum_down = weight_sums
    share_qkv, share_bqkv, share_out, share_up, share_bup, share_down = (
        lax.psum_scatter(
            sum_qkv.astype(jnp.bfloat16), "dp", scatter_dimension=0, tiled=True
        ).astype(jnp.float32),
        lax.psum_scatter(
            sum_bqkv.astype(jnp.bfloat16), "dp", scatter_dimension=1, tiled=True
        ).astype(jnp.float32),
        lax.psum_scatter(
            sum_out.astype(jnp.bfloat16), "dp", scatter_dimension=1, tiled=True
        ).astype(jnp.float32),
        lax.psum_scatter(sum_up.astype(jnp.bfloat16), "dp", scatter_dimension=0, tiled=True).astype(
            jnp.float32
        ),
        lax.psum_scatter(
            sum_bup.astype(jnp.bfloat16), "dp", scatter_dimension=1, tiled=True
        ).astype(jnp.float32),
        lax.psum_scatter(
            sum_down.astype(jnp.bfloat16), "dp", scatter_dimension=1, tiled=True
        ).astype(jnp.float32),
    )
    grad_local = lax.dynamic_slice_in_dim(jnp.stack(grad_list), 1 - section_index, MICRO, 0)
    gain_share, bias_share = (
        lax.psum_scatter(vector_sums[0], ("dp", "tensor"), scatter_dimension=1, tiled=True),
        lax.psum_scatter(vector_sums[1], ("dp", "tensor"), scatter_dimension=1, tiled=True),
    )
    return (
        acts_local[None],
        grad_local[None],
        gain_share[None],
        bias_share[None],
        share_qkv[None],
        share_bqkv[None],
        share_out[None],
        share_up[None],
        share_bup[None],
        share_down[None],
    )


def solution(mesh):
    placed = (
        P(None, "tensor", "dp", None),
        P(None, "tensor", "dp", None),
        P("section", None, ("dp", "tensor")),
        P("section", None, ("dp", "tensor")),
        P("section", "dp", "tensor"),
        P("section", "tensor", "dp"),
        P("section", "tensor", "dp"),
        P("section", "dp", "tensor"),
        P("section", "tensor", "dp"),
        P("section", "tensor", "dp"),
    )
    return jax.shard_map(
        local,
        mesh=mesh,
        in_specs=placed,
        out_specs=(
            P("section", None, "tensor", "dp", None),
            P("section", None, "tensor", "dp", None),
            P("section", None, ("dp", "tensor")),
            P("section", None, ("dp", "tensor")),
            P("section", "dp", "tensor"),
            P("section", "tensor", "dp"),
            P("section", "tensor", "dp"),
            P("section", "dp", "tensor"),
            P("section", "tensor", "dp"),
            P("section", "tensor", "dp"),
        ),
        check_vma=False,
    )
```

profile of v0, /device:TPU:0, one launch (start us, length us, event | category | flops | bytes accessed | tf_op | source)
XLA Modules:
  0.0 2164.0 jit_solution(13644089878775212534)
XLA Ops:
  12.2 47.4 %all-gather.2 = f32[1,4,1024]{1,0,2:T(1,128)S(1)} all-gather(f32[1,4,64]{1,0,2:T(1,128)S(1)} %copy.228), channel_id=4, replica_groups=mesh['section'=2,'dp'=4,'tensor'=4] {'dp','tensor'}, dimensions={2}, use_global_device_ids=true | all-gather | bytes 17408 | tf_op jit(solution)/shard_map/all_gather | solution.py:164
  59.6 21.7 %slice_reduce_fusion.11 = (f32[1024]{0:T(1024)S(1)}, f32[1024]{0:T(1024)S(1)}, f32[1024]{0:T(1024)S(1)}, f32[1024]{0:T(1024)S(1)}) fusion(f32[1,4,1024]{1,0,2:T(1,128)S(1)} %all-gather.2), kind=kLoop, calls=%fused_computation.917 | loop fusion | bytes 32768 | tf_op jit(solution)/shard_map/slice | solution.py:225
  81.4 5.9 all-gather.7
  87.5 35.0 %all-gather.1 = f32[1,2,1024]{1,0,2:T(1,128)S(1)} all-gather(f32[1,2,64]{1,0,2:T(1,128)S(1)} %copy.227), channel_id=3, replica_groups=mesh['section'=2,'dp'=4,'tensor'=4] {'dp','tensor'}, dimensions={2}, use_global_device_ids=true | all-gather | bytes 8704 | tf_op jit(solution)/shard_map/all_gather | solution.py:163
  122.6 7.2 slice_reduce_fusion.15
  130.2 6.0 all-gather.4
  137.2 7.3 all-gather.5
  156.5 14.3 fusion.5
  177.9 14.8 bitcast_dynamic-update-slice_fusion.9
  192.7 4.6 fusion.360
  200.2 76.0 %reduce-scatter.27.cloned.1.call-done = f32[256,1,1024]{2,0,1:T(8,128)} async-done(((f32[1024,1,1024]{2,0,1:T(8,128)}), f32[256,1,1024]{2,0,1:T(8,128)}) %reduce-scatter.27.cloned.1.call-update) | async-done | bytes 1048592 | tf_op jit(solution)/shard_map/reduce_scatter | solution.py:219
  281.8 10.8 collective-permute-done
  293.5 47.5 %all-gather.24.cloned.1.call-done = bf16[1024,1,1024]{2,0,1:T(8,128)(2,1)} async-done(((bf16[256,1,1024]{2,0,1:T(8,128)(2,1)}), bf16[1024,1,1024]{2,0,1:T(8,128)(2,1)}) %all-gather.24.cloned.1.call-update) | async-done | bytes 2097168 | tf_op jit(solution)/shard_map/all_gather | solution.py:187
  361.6 13.1 bitcast_dynamic-update-slice_fusion.8
  379.9 75.7 %reduce-scatter.29.cloned.1.call-done = f32[256,1,1024]{2,0,1:T(8,128)} async-done(((f32[1024,1,1024]{2,0,1:T(8,128)}), f32[256,1,1024]{2,0,1:T(8,128)}) %reduce-scatter.29.cloned.1.call-update) | async-done | bytes 1048592 | tf_op jit(solution)/shard_map/reduce_scatter | solution.py:219
  461.3 10.8 collective-permute-done.1
  474.5 47.1 %all-gather.26.cloned.1.call-done = bf16[1024,1,1024]{2,0,1:T(8,128)(2,1)} async-done(((bf16[256,1,1024]{2,0,1:T(8,128)(2,1)}), bf16[1024,1,1024]{2,0,1:T(8,128)(2,1)}) %all-gather.26.cloned.1.call-update) | async-done | bytes 2097168 | tf_op jit(solution)/shard_map/all_gather | solution.py:187
  542.2 13.1 bitcast_dynamic-update-slice_fusion.7
  560.5 75.7 %reduce-scatter.31.cloned.1.call-done = f32[256,1,1024]{2,0,1:T(8,128)} async-done(((f32[1024,1,1024]{2,0,1:T(8,128)}), f32[256,1,1024]{2,0,1:T(8,128)}) %reduce-scatter.31.cloned.1.call-update) | async-done | bytes 1048592 | tf_op jit(solution)/shard_map/reduce_scatter | solution.py:219
  641.9 10.8 collective-permute-done.2
  657.5 44.7 %all-gather.28.cloned.1.call-done = bf16[1024,1,1024]{2,0,1:T(8,128)(2,1)} async-done(((bf16[256,1,1024]{2,0,1:T(8,128)(2,1)}), bf16[1024,1,1024]{2,0,1:T(8,128)(2,1)}) %all-gather.28.cloned.1.call-update) | async-done | bytes 2097168 | tf_op jit(solution)/shard_map/all_gather | solution.py:187
  723.0 13.1 bitcast_dynamic-update-slice_fusion.6
  759.1 67.0 %reduce-scatter.33.cloned.1.call-done = f32[256,1,1024]{2,0,1:T(8,128)} async-done(((f32[1024,1,1024]{2,0,1:T(8,128)}), f32[256,1,1024]{2,0,1:T(8,128)}) %reduce-scatter.33.cloned.1.call-update) | async-done | bytes 1048592 | tf_op jit(solution)/shard_map/reduce_scatter | solution.py:219
  833.9 4.8 bitcast_dynamic-update-slice_fusion.3
  852.5 5.3 bitcast_dynamic-update-slice_fusion.2
  864.1 28.1 %all-gather.30.cloned.1.call-done = bf16[1024,1,1024]{2,0,1:T(8,128)(2,1)} async-done(((bf16[256,1,1024]{2,0,1:T(8,128)(2,1)}), bf16[1024,1,1024]{2,0,1:T(8,128)(2,1)}) %all-gather.30.cloned.1.call-update) | async-done | bytes 2097168 | tf_op jit(solution)/shard_map/all_gather | solution.py:187
  937.7 13.0 bitcast_dynamic-update-slice_fusion.5
  954.5 13.8 convert_reduce_fusion.9
  997.3 53.5 %reduce-scatter.37.cloned.1.call-done = bf16[256,1,2048]{2,0,1:T(8,128)(2,1)} async-done(((bf16[1024,1,2048]{2,0,1:T(8,128)(2,1)}), bf16[256,1,2048]{2,0,1:T(8,128)(2,1)}) %reduce-scatter.37.cloned.1.call-update) | async-done | bytes 1048592 | tf_op jit(solution)/shard_map/reduce_scatter | solution.py:317
  1061.3 14.0 collective-permute-done.4
  1082.1 5.6 fusion.780
  1087.8 35.8 %all-gather.32.cloned.1.call-done = bf16[1024,1,1024]{2,0,1:T(8,128)(2,1)} async-done(((bf16[256,1,1024]{2,0,1:T(8,128)(2,1)}), bf16[1024,1,1024]{2,0,1:T(8,128)(2,1)}) %all-gather.32.cloned.1.call-update) | async-done | bytes 2097168 | tf_op jit(solution)/shard_map/all_gather | solution.py:270
  1148.4 14.2 convert_reduce_fusion.8
  1169.4 75.7 %reduce-scatter.39.cloned.1.call-done = bf16[256,1,2048]{2,0,1:T(8,128)(2,1)} async-done(((bf16[1024,1,2048]{2,0,1:T(8,128)(2,1)}), bf16[256,1,2048]{2,0,1:T(8,128)(2,1)}) %reduce-scatter.39.cloned.1.call-update) | async-done | bytes 1048592 | tf_op jit(solution)/shard_map/reduce_scatter | solution.py:317
  1255.8 14.0 collective-permute-done.5
  1276.5 5.6 fusion.775
  1282.2 35.8 %all-gather.34.cloned.1.call-done = bf16[1024,1,1024]{2,0,1:T(8,128)(2,1)} async-done(((bf16[256,1,1024]{2,0,1:T(8,128)(2,1)}), bf16[1024,1,1024]{2,0,1:T(8,128)(2,1)}) %all-gather.34.cloned.1.call-update) | async-done | bytes 2097168 | tf_op jit(solution)/shard_map/all_gather | solution.py:270
  1343.6 14.2 convert_reduce_fusion.7
  1365.2 75.1 %reduce-scatter.41.cloned.1.call-done = bf16[256,1,2048]{2,0,1:T(8,128)(2,1)} async-done(((bf16[1024,1,2048]{2,0,1:T(8,128)(2,1)}), bf16[256,1,2048]{2,0,1:T(8,128)(2,1)}) %reduce-scatter.41.cloned.1.call-update) | async-done | bytes 1048592 | tf_op jit(solution)/shard_map/reduce_scatter | solution.py:317
  1451.0 14.0 collective-permute-done.6
  1471.6 5.6 fusion.770
  1477.2 36.0 %all-gather.36.cloned.1.call-done = bf16[1024,1,1024]{2,0,1:T(8,128)(2,1)} async-done(((bf16[256,1,1024]{2,0,1:T(8,128)(2,1)}), bf16[1024,1,1024]{2,0,1:T(8,128)(2,1)}) %all-gather.36.cloned.1.call-update) | async-done | bytes 2097168 | tf_op jit(solution)/shard_map/all_gather | solution.py:270
  1539.1 13.6 convert_reduce_fusion.6
  1560.1 75.1 %reduce-scatter.43.cloned.1.call-done = bf16[256,1,2048]{2,0,1:T(8,128)(2,1)} async-done(((bf16[1024,1,2048]{2,0,1:T(8,128)(2,1)}), bf16[256,1,2048]{2,0,1:T(8,128)(2,1)}) %reduce-scatter.43.cloned.1.call-update) | async-done | bytes 1048592 | tf_op jit(solution)/shard_map/reduce_scatter | solution.py:317
  1653.6 6.7 collective-permute-done.7
  1667.0 5.0 fusion.628
  1672.0 5.7 fusion.765
  1692.5 5.3 fusion.294
  1697.8 5.3 fusion.292
  1705.8 5.3 fusion.290
  1724.5 4.7 multiply_reduce_fusion
  1740.5 15.1 convert_reduce_fusion.5
  1768.0 5.4 add_convert_fusion.2
  1788.9 7.6 add_convert_fusion.1
  1805.4 4.4 fusion.270
  1809.8 4.4 fusion.268
  1814.3 8.3 add_convert_fusion
  1838.7 17.7 reduce-scatter.49.cloned.1.call-done
  1858.1 28.8 %reduce-scatter.47.cloned.1.call-done = bf16[256,768]{1,0:T(8,128)(2,1)} async-done(((bf16[1024,768]{1,0:T(8,128)(2,1)}), bf16[256,768]{1,0:T(8,128)(2,1)}) %reduce-scatter.47.cloned.1.call-update) | async-done | bytes 393232 | tf_op jit(solution)/shard_map/reduce_scatter | solution.py:357
  1888.8 31.7 %reduce-scatter.51.cloned.1.call-done = bf16[256,1024]{1,0:T(8,128)(2,1)} async-done(((bf16[1024,1024]{1,0:T(8,128)(2,1)}), bf16[256,1024]{1,0:T(8,128)(2,1)}) %reduce-scatter.51.cloned.1.call-update) | async-done | bytes 524304 | tf_op jit(solution)/shard_map/reduce_scatter | solution.py:366
  1922.6 31.6 %reduce-scatter.53.cloned.1.call-done = bf16[1024,256]{1,0:T(8,128)(2,1)} async-done(((bf16[1024,1024]{1,0:T(8,128)(2,1)}), bf16[1024,256]{1,0:T(8,128)(2,1)}) %reduce-scatter.53.cloned.1.call-update) | async-done | bytes 524304 | tf_op jit(solution)/shard_map/reduce_scatter | solution.py:372
  1956.4 76.9 %reduce-scatter.45.cloned.1.call-done = bf16[256,1,2048]{2,0,1:T(8,128)(2,1)} async-done(((bf16[1024,1,2048]{2,0,1:T(8,128)(2,1)}), bf16[256,1,2048]{2,0,1:T(8,128)(2,1)}) %reduce-scatter.45.cloned.1.call-update) | async-done | bytes 1048592 | tf_op jit(solution)/shard_map/reduce_scatter | solution.py:317
  2046.9 49.8 %reduce-scatter.55.cloned.1.call-done = f32[64,2]{1,0:T(8,128)} async-done(((f32[1024,2]{1,0:T(8,128)}), f32[64,2]{1,0:T(8,128)}) %reduce-scatter.55.cloned.1.call-update) | async-done | bytes 528
  2098.1 57.4 %reduce-scatter.57.cloned.1.call-done = f32[64,4]{1,0:T(8,128)} async-done(((f32[1024,4]{1,0:T(8,128)}), f32[64,4]{1,0:T(8,128)}) %reduce-scatter.57.cloned.1.call-update) | async-done | bytes 1040
  (967 shorter events, 545.4 us)
Async XLA Ops:
  7.2 122.9 %copy-start.206 = (bf16[1,4,48]{2,1,0:T(4,128)(2,1)S(1)}, bf16[1,4,48]{2,1,0:T(4,128)(2,1)}, u32[]{:S(2)}) copy-start(bf16[1,4,48]{2,1,0:T(4,128)(2,1)} %param.75) | copy-start | bytes 1156
  7.2 137.3 %all-gather.40.cloned.1.call-start = ((), (), s32[]{:S(2)}) async-start(), calls=%async_computation.40 | async-start | bytes 2621440 | tf_op jit(solution)/shard_map/all_gather | solution.py:187
  7.3 129.9 %copy-start.117 = (bf16[1,256,256]{2,1,0:T(8,128)(2,1)S(1)}, bf16[1,256,256]{2,1,0:T(8,128)(2,1)}, u32[]{:S(2)}) copy-start(bf16[1,256,256]{2,1,0:T(8,128)(2,1)} %param.76) | copy-start | bytes 393220
  9.2 139.8 %all-gather.42.cloned.1.call-start = ((), (), s32[]{:S(2)}) async-start(), calls=%async_computation.41 | async-start | bytes 1966080 | tf_op jit(solution)/shard_map/all_gather | solution.py:167
  10.0 167.9 %all-gather.44.cloned.1.call-start = ((), (), s32[]{:S(2)}) async-start(), calls=%async_computation.42 | async-start | bytes 2621440 | tf_op jit(solution)/shard_map/all_gather | solution.py:170
  10.7 182.0 %all-gather.46.cloned.1.call-start = ((), (), s32[]{:S(2)}) async-start(), calls=%async_computation.43 | async-start | bytes 2621440 | tf_op jit(solution)/shard_map/all_gather | solution.py:172
  11.3 264.9 %reduce-scatter.27.cloned.1.call-start = ((), (), s32[]{:S(2)}) async-start(), calls=%async_computation.18 | async-start | bytes 5242880 | tf_op jit(solution)/shard_map/reduce_scatter | solution.py:219
  81.3 554.9 %copy-start.111 = (f32[1024]{0:T(1024)}, f32[1024]{0:T(1024)S(1)}, u32[]{:S(2)}) copy-start(f32[1024]{0:T(1024)S(1)} %get-tuple-element.395) | copy-start | bytes 12292
  81.3 554.9 %copy-start.113 = (f32[1024]{0:T(1024)}, f32[1024]{0:T(1024)S(1)}, u32[]{:S(2)}) copy-start(f32[1024]{0:T(1024)S(1)} %get-tuple-element.398) | copy-start | bytes 12292
  87.4 635.3 %copy-start.115 = (f32[1024]{0:T(1024)}, f32[1024]{0:T(1024)S(1)}, u32[]{:S(2)}) copy-start(f32[1024]{0:T(1024)S(1)} %bitcast_convert_fusion.5) | copy-start | bytes 12292
  129.7 1512.1 %copy-start.61 = (f32[1024]{0:T(1024)}, f32[1024]{0:T(1024)S(1)}, u32[]{:S(2)}) copy-start(f32[1024]{0:T(1024)S(1)} %get-tuple-element.399) | copy-start | bytes 12292
  129.7 1512.1 %copy-start.63 = (f32[1024]{0:T(1024)}, f32[1024]{0:T(1024)S(1)}, u32[]{:S(2)}) copy-start(f32[1024]{0:T(1024)S(1)} %get-tuple-element.400) | copy-start | bytes 12292
  144.5 593.9 %copy-start.4 = (bf16[1,256,1024]{2,1,0:T(8,128)(2,1)}, bf16[1,256,1024]{2,1,0:T(8,128)(2,1)S(1)}, u32[]{:S(2)}) copy-start(bf16[1,256,1024]{2,1,0:T(8,128)(2,1)S(1)} %all-gather.5) | copy-start | bytes 1572868
  200.1 140.9 %all-gather.24.cloned.1.call-start = ((), (), s32[]{:S(2)}) async-start(), calls=%async_computation.19 | async-start | bytes 2621440 | tf_op jit(solution)/shard_map/all_gather | solution.py:187
  278.4 14.3 collective-permute-start
  293.5 162.2 %reduce-scatter.29.cloned.1.call-start = ((), (), s32[]{:S(2)}) async-start(), calls=%async_computation.20 | async-start | bytes 5242880 | tf_op jit(solution)/shard_map/reduce_scatter | solution.py:219
  379.9 141.7 %all-gather.26.cloned.1.call-start = ((), (), s32[]{:S(2)}) async-start(), calls=%async_computation.21 | async-start | bytes 2621440 | tf_op jit(solution)/shard_map/all_gather | solution.py:187
  457.9 14.2 collective-permute-start.1
  474.0 162.2 %reduce-scatter.31.cloned.1.call-start = ((), (), s32[]{:S(2)}) async-start(), calls=%async_computation.22 | async-start | bytes 5242880 | tf_op jit(solution)/shard_map/reduce_scatter | solution.py:219
  560.5 141.8 %all-gather.28.cloned.1.call-start = ((), (), s32[]{:S(2)}) async-start(), calls=%async_computation.23 | async-start | bytes 2621440 | tf_op jit(solution)/shard_map/all_gather | solution.py:187
  638.5 14.2 collective-permute-start.2
  654.7 93.7 %all-gather.48.cloned.1.call-start = ((), (), s32[]{:S(2)}) async-start(), calls=%async_computation.44 | async-start | bytes 2621440 | tf_op jit(solution)/shard_map/all_gather | solution.py:270
  657.3 168.8 %reduce-scatter.33.cloned.1.call-start = ((), (), s32[]{:S(2)}) async-start(), calls=%async_computation.24 | async-start | bytes 5242880 | tf_op jit(solution)/shard_map/reduce_scatter | solution.py:219
  741.2 151.0 %all-gather.30.cloned.1.call-start = ((), (), s32[]{:S(2)}) async-start(), calls=%async_computation.25 | async-start | bytes 2621440 | tf_op jit(solution)/shard_map/all_gather | solution.py:187
  828.4 14.2 collective-permute-start.3
  844.6 206.2 %reduce-scatter.37.cloned.1.call-start = ((), (), s32[]{:S(2)}) async-start(), calls=%async_computation.27 | async-start | bytes 5242880 | tf_op jit(solution)/shard_map/reduce_scatter | solution.py:317
  975.0 148.6 %all-gather.32.cloned.1.call-start = ((), (), s32[]{:S(2)}) async-start(), calls=%async_computation.28 | async-start | bytes 2621440 | tf_op jit(solution)/shard_map/all_gather | solution.py:270
  1060.0 15.2 collective-permute-start.4
  1077.9 167.2 %reduce-scatter.39.cloned.1.call-start = ((), (), s32[]{:S(2)}) async-start(), calls=%async_computation.29 | async-start | bytes 5242880 | tf_op jit(solution)/shard_map/reduce_scatter | solution.py:317
  1169.3 148.7 %all-gather.34.cloned.1.call-start = ((), (), s32[]{:S(2)}) async-start(), calls=%async_computation.30 | async-start | bytes 2621440 | tf_op jit(solution)/shard_map/all_gather | solution.py:270
  1254.3 15.4 collective-permute-start.5
  1272.3 168.0 %reduce-scatter.41.cloned.1.call-start = ((), (), s32[]{:S(2)}) async-start(), calls=%async_computation.31 | async-start | bytes 5242880 | tf_op jit(solution)/shard_map/reduce_scatter | solution.py:317
  1364.6 148.6 %all-gather.36.cloned.1.call-start = ((), (), s32[]{:S(2)}) async-start(), calls=%async_computation.32 | async-start | bytes 2621440 | tf_op jit(solution)/shard_map/all_gather | solution.py:270
  1449.6 15.4 collective-permute-start.6
  1467.5 167.7 %reduce-scatter.43.cloned.1.call-start = ((), (), s32[]{:S(2)}) async-start(), calls=%async_computation.33 | async-start | bytes 5242880 | tf_op jit(solution)/shard_map/reduce_scatter | solution.py:317
  1559.5 154.4 %all-gather.38.cloned.1.call-start = ((), (), s32[]{:S(2)}) async-start(), calls=%async_computation.34 | async-start | bytes 2621440 | tf_op jit(solution)/shard_map/all_gather | solution.py:270
  1644.7 15.7 collective-permute-start.7
  1663.2 168.7 %reduce-scatter.35.cloned.1.call-start = ((), (), s32[]{:S(2)}) async-start(), calls=%async_computation.26 | async-start | bytes 5242880 | tf_op jit(solution)/shard_map/reduce_scatter | solution.py:219
  1682.9 153.1 %reduce-scatter.59.cloned.1.call-start = ((), (), s32[]{:S(2)}) async-start(), calls=%async_computation.47 | async-start | bytes 61440
  1740.3 97.1 %reduce-scatter.61.cloned.1.call-start = ((), (), s32[]{:S(2)}) async-start(), calls=%async_computation.48 | async-start | bytes 40960
  1756.4 100.1 %reduce-scatter.49.cloned.1.call-start = ((), (), s32[]{:S(2)}) async-start(), calls=%async_computation.37 | async-start | bytes 655360 | tf_op jit(solution)/shard_map/reduce_scatter | solution.py:363
  1762.5 124.3 %reduce-scatter.47.cloned.1.call-start = ((), (), s32[]{:S(2)}) async-start(), calls=%async_computation.36 | async-start | bytes 1966080 | tf_op jit(solution)/shard_map/reduce_scatter | solution.py:357
  1773.3 147.1 %reduce-scatter.51.cloned.1.call-start = ((), (), s32[]{:S(2)}) async-start(), calls=%async_computation.38 | async-start | bytes 2621440 | tf_op jit(solution)/shard_map/reduce_scatter | solution.py:366
  1796.5 157.7 %reduce-scatter.53.cloned.1.call-start = ((), (), s32[]{:S(2)}) async-start(), calls=%async_computation.39 | async-start | bytes 2621440 | tf_op jit(solution)/shard_map/reduce_scatter | solution.py:372
  1822.6 210.7 %reduce-scatter.45.cloned.1.call-start = ((), (), s32[]{:S(2)}) async-start(), calls=%async_computation.35 | async-start | bytes 5242880 | tf_op jit(solution)/shard_map/reduce_scatter | solution.py:317
  1831.2 265.5 %reduce-scatter.55.cloned.1.call-start = ((), (), s32[]{:S(2)}) async-start(), calls=%async_computation.45 | async-start | bytes 557056
  1836.0 198.8 %copy-start.62 = (f32[1024]{0:T(1024)S(1)}, f32[1024]{0:T(1024)}, u32[]{:S(2)}) copy-start(f32[1024]{0:T(1024)} %copy-done.61) | copy-start | bytes 12292
  1836.0 198.8 %copy-start.64 = (f32[1024]{0:T(1024)S(1)}, f32[1024]{0:T(1024)}, u32[]{:S(2)}) copy-start(f32[1024]{0:T(1024)} %copy-done.63) | copy-start | bytes 12292
  1956.2 82.4 %copy-start.191 = (f32[1024]{0:T(1024)S(1)}, f32[1024]{0:T(1024)}, u32[]{:S(2)}) copy-start(f32[1024]{0:T(1024)} %get-tuple-element.338) | copy-start | bytes 12292
  1956.3 82.4 %copy-start.192 = (f32[1024]{0:T(1024)S(1)}, f32[1024]{0:T(1024)}, u32[]{:S(2)}) copy-start(f32[1024]{0:T(1024)} %get-tuple-element.339) | copy-start | bytes 12292
  1956.3 83.6 %copy-start.177 = (f32[1024]{0:T(1024)S(1)}, f32[1024]{0:T(1024)}, u32[]{:S(2)}) copy-start(f32[1024]{0:T(1024)} %get-tuple-element.429) | copy-start | bytes 12292
  1956.3 83.6 %copy-start.178 = (f32[1024]{0:T(1024)S(1)}, f32[1024]{0:T(1024)}, u32[]{:S(2)}) copy-start(f32[1024]{0:T(1024)} %get-tuple-element.390) | copy-start | bytes 12292
  1956.3 83.6 %copy-start.179 = (f32[1024]{0:T(1024)S(1)}, f32[1024]{0:T(1024)}, u32[]{:S(2)}) copy-start(f32[1024]{0:T(1024)} %get-tuple-element.391) | copy-start | bytes 12292
  1956.3 83.6 %copy-start.180 = (f32[1024]{0:T(1024)S(1)}, f32[1024]{0:T(1024)}, u32[]{:S(2)}) copy-start(f32[1024]{0:T(1024)} %get-tuple-element.427) | copy-start | bytes 12292
  1956.3 83.6 %copy-start.183 = (f32[1024]{0:T(1024)S(1)}, f32[1024]{0:T(1024)}, u32[]{:S(2)}) copy-start(f32[1024]{0:T(1024)} %get-tuple-element.385) | copy-start | bytes 12292
  1956.3 83.6 %copy-start.184 = (f32[1024]{0:T(1024)S(1)}, f32[1024]{0:T(1024)}, u32[]{:S(2)}) copy-start(f32[1024]{0:T(1024)} %get-tuple-element.386) | copy-start | bytes 12292
  1956.3 83.6 %copy-start.185 = (f32[1024]{0:T(1024)S(1)}, f32[1024]{0:T(1024)}, u32[]{:S(2)}) copy-start(f32[1024]{0:T(1024)} %get-tuple-element.425) | copy-start | bytes 12292
  1956.4 83.6 %copy-start.188 = (f32[1024]{0:T(1024)S(1)}, f32[1024]{0:T(1024)}, u32[]{:S(2)}) copy-start(f32[1024]{0:T(1024)} %get-tuple-element.380) | copy-start | bytes 12292
  1956.4 83.6 %copy-start.189 = (f32[1024]{0:T(1024)S(1)}, f32[1024]{0:T(1024)}, u32[]{:S(2)}) copy-start(f32[1024]{0:T(1024)} %get-tuple-element.381) | copy-start | bytes 12292
  1956.4 83.6 %copy-start.190 = (f32[1024]{0:T(1024)S(1)}, f32[1024]{0:T(1024)}, u32[]{:S(2)}) copy-start(f32[1024]{0:T(1024)} %get-tuple-element.423) | copy-start | bytes 12292
  1956.4 83.6 %copy-start.193 = (f32[1024]{0:T(1024)S(1)}, f32[1024]{0:T(1024)}, u32[]{:S(2)}) copy-start(f32[1024]{0:T(1024)} %get-tuple-element.375) | copy-start | bytes 12292
  1956.4 83.6 %copy-start.194 = (f32[1024]{0:T(1024)S(1)}, f32[1024]{0:T(1024)}, u32[]{:S(2)}) copy-start(f32[1024]{0:T(1024)} %get-tuple-element.376) | copy-start | bytes 12292
  1956.4 83.6 %copy-start.197 = (f32[1024]{0:T(1024)S(1)}, f32[1024]{0:T(1024)}, u32[]{:S(2)}) copy-start(f32[1024]{0:T(1024)} %get-tuple-element.421) | copy-start | bytes 12292
  2039.8 115.7 %reduce-scatter.57.cloned.1.call-start = ((), (), s32[]{:S(2)}) async-start(), calls=%async_computation.46 | async-start | bytes 557056
  (230 other events, 2202.1 us)
Sparse Core Ops, SparseCore 0:
  10.2 56.8 all-gather.39
  68.6 19.5 all-gather.41
  89.8 23.6 all-gather.43
  114.8 23.3 all-gather.45
  200.3 75.8 reduce-scatter.26
  293.6 47.4 all-gather.23
  380.0 75.5 reduce-scatter.28
  474.2 47.4 all-gather.25
  560.6 75.5 reduce-scatter.30
  654.8 47.4 all-gather.27
  703.8 44.4 all-gather.47
  750.5 75.5 reduce-scatter.32
  844.7 47.4 all-gather.29
  975.1 75.5 reduce-scatter.36
  1078.0 45.5 all-gather.31
  1169.5 75.5 reduce-scatter.38
  1272.4 45.5 all-gather.33
  1364.7 75.5 reduce-scatter.40
  1467.7 45.4 all-gather.35
  1559.6 75.5 reduce-scatter.42
  1663.3 45.4 all-gather.37
  1711.1 75.5 reduce-scatter.34
  1789.7 20.0 reduce-scatter.58
  1812.1 19.5 reduce-scatter.60
  1834.7 21.6 reduce-scatter.48
  1858.8 27.9 reduce-scatter.46
  1889.2 31.1 reduce-scatter.50
  1923.0 31.1 reduce-scatter.52
  1956.4 76.7 reduce-scatter.44
  2040.0 56.7 reduce-scatter.54
  2100.3 55.2 reduce-scatter.56
where the time goes:
time: 2170 us; the launch traced here: 2160 us
  waiting for transfers between devices  1230 us (57%)
  matrix products  471 us (22%)
  other arithmetic  220 us (10%)
  blocking collectives  102 us (5%)
  local copies, waits for them, and re-layouts  98.2 us (5%)
  starting transfers between devices  23.6 us (1%)
    reduce_scatter x5, waiting for transfers between devices, local(): lax.psum_scatter(joined.reshape(lax.axis_size('tensor') * local_len, seq_...  356 us
    reduce_scatter x5, waiting for transfers between devices, local(): lax.psum_scatter(summed.reshape(lax.axis_size('tensor') * local_len, seq_...  294 us
    all_gather x5, waiting for transfers between devices, local(): forward_gathered = lax.all_gather(inputs, 'tensor', axis=0, tiled=True)  167 us
    unnamed x35, waiting for transfers between devices  110 us
    all_gather x5, waiting for transfers between devices, local(): upstream_rows = lax.all_gather(upstream, 'tensor', axis=0, tiled=True)  108 us
    ppermute x8, waiting for transfers between devices, from_behind(): return lax.ppermute(value, axis, pairs)  85 us
    dot_general x5, matrix products, local(): jnp.dot(flat_grad, mat_down.T, preferred_element_type=jnp.float32)  70.9 us
    dot_general x5, matrix products, local(): jnp.dot(forward_flat_mlp, mat_up, preferred_element_type=jnp.float32)  67.1 us
  transfers between devices with their start and end apart: 39, of which 31 were waited for; matrix products, arithmetic and copies ran while one was open for 18% of the time, Pallas kernels for 0%

commit v1 on v0

v1 whole, which is shorter than its diff:
```python
import math

import jax
import jax.numpy as jnp
from jax import lax
from jax.experimental import pallas as pl
from jax.experimental.pallas import tpu as pltpu
from jax.sharding import Mesh
from jax.sharding import PartitionSpec as P

ROT = 16
NORM_EPS = 1e-05
ROPE_BASE = 10000.0
MASK_FILL = -1e30
BLOCK = 256
PAIR = 2
F32 = jnp.float32
BF16 = jnp.bfloat16


def rotation_tables(length, head_dim):
    half = ROT // 2
    frequency = jnp.exp(jnp.arange(half, dtype=F32) * (-2.0 * math.log(ROPE_BASE) / ROT))
    angles = jnp.arange(length, dtype=F32)[:, None] * frequency[None, :]
    cosine, sine = jnp.cos(angles), jnp.sin(angles)
    zero = jnp.zeros_like(sine)
    rest = jnp.zeros((length, head_dim - ROT), F32)
    keep_part = jnp.concatenate([cosine, cosine, rest + 1.0], axis=1)
    ahead_part = jnp.concatenate([-sine, zero, rest], axis=1)
    behind_part = jnp.concatenate([zero, sine, rest], axis=1)
    plain = jnp.zeros((length, head_dim), F32)

    def widen(part, value_part):
        return jnp.concatenate([part, part, value_part] * PAIR, axis=1)

    return (
        widen(keep_part, plain + 1.0),
        widen(ahead_part, plain),
        widen(behind_part, plain),
    )


def turn(values, keep, ahead, behind, sign):
    width = values.shape[1]
    half = ROT // 2
    moved = pltpu.roll(values, width - half, 1) * ahead + pltpu.roll(values, half, 1) * behind
    return values * keep + moved * sign


def rows_dot(left, right):
    return lax.dot_general(left, right, (((1,), (1,)), ((), ())), preferred_element_type=F32)


def attend_kernel(qkv_ref, keep_ref, ahead_ref, behind_ref, out_ref):
    length = qkv_ref.shape[1]
    head_dim = out_ref.shape[1] // PAIR
    block = min(BLOCK, length)
    turned = turn(qkv_ref[0].astype(F32), keep_ref[...], ahead_ref[...], behind_ref[...], 1.0)
    scale = head_dim ** (-0.5)
    parts = []
    for head in range(PAIR):
        base = head * 3 * head_dim
        queries = (turned[:, base : base + head_dim].astype(BF16).astype(F32) * scale).astype(BF16)
        key_rows = turned[:, base + head_dim : base + 2 * head_dim].astype(BF16)
        val_rows = turned[:, base + 2 * head_dim : base + 3 * head_dim].astype(BF16)
        parts.append((queries, key_rows, val_rows))
    row = lax.broadcasted_iota(jnp.int32, (block, block), 0)
    col = lax.broadcasted_iota(jnp.int32, (block, block), 1)
    allowed = col <= row
    for start in range(0, length, block):
        stop = start + block
        outs = []
        for queries, key_rows, val_rows in parts:
            scores = rows_dot(queries[start:stop], key_rows[:stop])
            edge = jnp.where(allowed, scores[:, start:], MASK_FILL)
            if start:
                scores = jnp.concatenate([scores[:, :start], edge], axis=1)
            else:
                scores = edge
            highest = jnp.max(scores, axis=1, keepdims=True)
            exponent = jnp.exp(scores - highest)
            inverse = 1.0 / jnp.sum(exponent, axis=1, keepdims=True)
            probability = (exponent * inverse).astype(BF16)
            outs.append(jnp.dot(probability, val_rows[:stop], preferred_element_type=F32))
        out_ref[start:stop, :] = jnp.concatenate(outs, axis=1).astype(BF16)


def attend_back_kernel(qkv_ref, dctx_ref, keep_ref, ahead_ref, behind_ref, out_ref, total):
    length = qkv_ref.shape[1]
    head_dim = dctx_ref.shape[1] // PAIR
    block = min(BLOCK, length)
    turned = turn(qkv_ref[0].astype(F32), keep_ref[...], ahead_ref[...], behind_ref[...], 1.0)
    scale = head_dim ** (-0.5)
    key_pos = lax.broadcasted_iota(jnp.int32, (block, block), 0)
    row_pos = lax.broadcasted_iota(jnp.int32, (block, block), 1)
    allowed = key_pos <= row_pos
    parts = []
    for head in range(PAIR):
        base = head * 3 * head_dim
        queries = (turned[:, base : base + head_dim].astype(BF16).astype(F32) * scale).astype(BF16)
        key_rows = turned[:, base + head_dim : base + 2 * head_dim].astype(BF16)
        val_rows = turned[:, base + 2 * head_dim : base + 3 * head_dim].astype(BF16)
        d_rows = dctx_ref[:, head * head_dim : (head + 1) * head_dim]
        parts.append((base, queries, key_rows, val_rows, d_rows))
    for start in reversed(range(0, length, block)):
        stop = start + block
        for base, queries, key_rows, val_rows, d_rows in parts:
            query_block = queries[start:stop]
            d_block = d_rows[start:stop]
            scores = rows_dot(key_rows[:stop], query_block)
            edge = jnp.where(allowed, scores[start:], MASK_FILL)
            if start:
                scores = jnp.concatenate([scores[:start], edge], axis=0)
            else:
                scores = edge
            highest = jnp.max(scores, axis=0, keepdims=True)
            exponent = jnp.exp(scores - highest)
            inverse = 1.0 / jnp.sum(exponent, axis=0, keepdims=True)
            probability = exponent * inverse
            d_prob = rows_dot(val_rows[:stop], d_block)
            delta = jnp.sum(probability * d_prob, axis=0, keepdims=True)
            d_scores = (probability * (d_prob - delta)).astype(BF16)
            d_keys = jnp.dot(d_scores, query_block, preferred_element_type=F32)
            d_vals = jnp.dot(probability.astype(BF16), d_block, preferred_element_type=F32)
            d_queries = lax.dot_general(
                key_rows[:stop], d_scores, (((0,), (0,)), ((), ())), preferred_element_type=F32
            )
            total[start:stop, base : base + head_dim] = d_queries.T * scale
            key_at = slice(base + head_dim, base + 2 * head_dim)
            val_at = slice(base + 2 * head_dim, base + 3 * head_dim)
            if stop == length:
                total[:stop, key_at] = d_keys
                total[:stop, val_at] = d_vals
            else:
                total[:stop, key_at] = total[:stop, key_at] + d_keys
                total[:stop, val_at] = total[:stop, val_at] + d_vals
    out_ref[0] = turn(total[...], keep_ref[...], ahead_ref[...], behind_ref[...], -1.0).astype(BF16)


def attention(qkv, tables, length, head_dim):
    groups, rows, width = qkv.shape
    wide = PAIR * 3 * head_dim
    pairs = width // wide
    table = pl.BlockSpec((length, wide), lambda t, n, p: (0, 0))
    work = groups * rows * pairs * PAIR * length * head_dim
    return pl.pallas_call(
        attend_kernel,
        out_shape=jax.ShapeDtypeStruct((rows, groups * pairs * PAIR * head_dim), BF16),
        grid=(groups, rows // length, pairs),
        in_specs=[pl.BlockSpec((1, length, wide), lambda t, n, p: (t, n, p))] + [table] * 3,
        out_specs=pl.BlockSpec((length, PAIR * head_dim), lambda t, n, p: (n, t * pairs + p)),
        cost_estimate=pl.CostEstimate(
            flops=4 * work, bytes_accessed=qkv.size * 3, transcendentals=work // head_dim
        ),
        name="attend",
    )(qkv, *tables)


def attention_back(qkv, d_context, tables, length, head_dim):
    groups, rows, width = qkv.shape
    wide = PAIR * 3 * head_dim
    pairs = width // wide
    table = pl.BlockSpec((length, wide), lambda t, n, p: (0, 0))
    work = groups * rows * pairs * PAIR * length * head_dim
    return pl.pallas_call(
        attend_back_kernel,
        out_shape=jax.ShapeDtypeStruct(qkv.shape, BF16),
        grid=(groups, rows // length, pairs),
        in_specs=[
            pl.BlockSpec((1, length, wide), lambda t, n, p: (t, n, p)),
            pl.BlockSpec((length, PAIR * head_dim), lambda t, n, p: (n, t * pairs + p)),
        ]
        + [table] * 3,
        out_specs=pl.BlockSpec((1, length, wide), lambda t, n, p: (t, n, p)),
        scratch_shapes=[pltpu.VMEM((length, wide), F32)],
        cost_estimate=pl.CostEstimate(
            flops=10 * work, bytes_accessed=qkv.size * 5, transcendentals=work // head_dim
        ),
        name="attend_back",
    )(qkv, d_context, *tables)


def product(equation, left, right):
    return jnp.einsum(equation, left, right, preferred_element_type=F32)


def statistics(values):
    average = jnp.mean(values, axis=-1, keepdims=True)
    centred = values - average
    variance = jnp.mean(centred * centred, axis=-1, keepdims=True)
    inverse = lax.rsqrt(variance + NORM_EPS)
    return centred * inverse, inverse


def forward(inputs, params, tables, length, head_dim):
    gains, shifts, mat_qkv, bias_qkv, mat_out, mat_up, bias_up, mat_down = params
    values = inputs.astype(F32)
    scaled, _ = statistics(values)
    normed_attn = (scaled * gains[0] + shifts[0]).astype(BF16)
    normed_mlp = (scaled * gains[1] + shifts[1]).astype(BF16)
    qkv = (product("sk,tke->tse", normed_attn, mat_qkv) + bias_qkv[:, None, :]).astype(BF16)
    context = attention(qkv, tables, length, head_dim)
    raised = product("sk,tke->ste", normed_mlp, mat_up) + bias_up
    below = 0.5 * lax.erf(raised * math.sqrt(0.5)) + 0.5
    active = (raised * below).astype(BF16)
    slope = (below + raised * jnp.exp(-0.5 * raised * raised) * (1.0 / math.sqrt(2.0 * math.pi))).astype(BF16)
    rows = inputs.shape[0]
    active = active.reshape(rows, -1)
    slope = slope.reshape(rows, -1)
    summed = product("sk,bkn->sbn", context, mat_out) + product("sk,bkn->sbn", active, mat_down)
    result = values + summed.reshape(rows, -1) + (shifts[2] + shifts[3])
    return result.astype(BF16), (normed_attn, normed_mlp, qkv, context, active, slope)


def backward(inputs, upstream, params, stash, tables, length, head_dim):
    gains, shifts, mat_qkv, bias_qkv, mat_out, mat_up, bias_up, mat_down = params
    normed_attn, normed_mlp, qkv, context, active, slope = stash
    rows = inputs.shape[0]
    pieces = mat_out.shape[0]
    groups = mat_qkv.shape[0]
    split = upstream.reshape(rows, pieces, -1)
    d_active = product("sbn,bkn->sk", split, mat_down)
    d_up = (d_active * slope.astype(F32)).astype(BF16)
    d_context = product("sbn,bkn->sk", split, mat_out).astype(BF16)
    d_up_split = d_up.reshape(rows, groups, -1)
    grad_down = product("sk,sbn->bkn", active, split)
    grad_up = product("sk,ste->tke", normed_mlp, d_up_split)
    d_qkv = attention_back(qkv, d_context, tables, length, head_dim)
    grad_out = product("sk,sbn->bkn", context, split)
    grad_qkv = product("sk,tse->tke", normed_attn, d_qkv)
    d_attn = product("tse,tke->sk", d_qkv, mat_qkv)
    d_mlp = product("ste,tke->sk", d_up_split, mat_up)
    scaled, inverse = statistics(inputs.astype(F32))
    d_scaled = d_attn * gains[0] + d_mlp * gains[1]
    term = inverse * (
        d_scaled
        - jnp.mean(d_scaled, axis=-1, keepdims=True)
        - scaled * jnp.mean(d_scaled * scaled, axis=-1, keepdims=True)
    )
    upstream_float = upstream.astype(F32)
    d_inputs = (upstream_float + term).astype(BF16)
    out_shift = jnp.sum(upstream_float, axis=0)
    small = (
        jnp.stack([jnp.sum(d_attn * scaled, axis=0), jnp.sum(d_mlp * scaled, axis=0)]),
        jnp.stack([jnp.sum(d_attn, axis=0), jnp.sum(d_mlp, axis=0), out_shift, out_shift]),
        jnp.sum(d_qkv.astype(F32), axis=1),
        jnp.sum(d_up_split.astype(F32), axis=0),
    )
    return d_inputs, (grad_qkv, grad_out, grad_up, grad_down), small


def swap_pairs(axis):
    return [(0, 1), (1, 0)]


def gather_stack(value, axis):
    if lax.axis_size(axis) == 2:
        other = lax.ppermute(value, axis, swap_pairs(axis))
        first = lax.axis_index(axis) == 0
        return jnp.stack([jnp.where(first, value, other), jnp.where(first, other, value)])
    return lax.all_gather(value, axis, axis=0, tiled=False)


def halve(value, axis):
    mine = lax.axis_index(axis)
    kept = lax.dynamic_index_in_dim(value, mine, 0, keepdims=False)
    sent = lax.dynamic_index_in_dim(value, 1 - mine, 0, keepdims=False).astype(BF16)
    came = lax.ppermute(sent, axis, swap_pairs(axis))
    return kept.astype(F32) + came.astype(F32)


def scatter_sum(value, axis):
    if lax.axis_size(axis) == 2:
        return halve(value, axis)
    return lax.psum_scatter(value.astype(BF16), axis, scatter_dimension=0, tiled=False).astype(F32)


def local(acts_in, cotangent, norm_gains, vec_bias, w_qkv, b_qkv, w_out, w_up, b_up, w_down):
    micro, local_len, local_seqs, width = acts_in.shape
    count_t = lax.axis_size("tensor")
    count_x = lax.axis_size("x")
    count_c = lax.axis_size("core")
    sections = lax.axis_size("section")
    section_index = lax.axis_index("section")
    length = local_len * count_t
    slots = -(-micro // count_t)
    padding = slots * count_t - micro
    head_dim = b_qkv.shape[2] * count_x * count_c // 3
    seqs = slots * local_seqs
    rows = seqs * length

    def features_in(value):
        lead = value.shape[:-1]
        value = value.reshape(*lead, count_x, count_c, -1)
        return jnp.swapaxes(value, -3, -2).reshape(*lead, width)

    def features_out(value):
        lead = value.shape[:-1]
        value = value.reshape(*lead, count_c, count_x, -1)
        return jnp.swapaxes(value, -3, -2).reshape(*lead, width)

    def collect(value):
        value = features_in(value)
        if padding:
            value = jnp.pad(value, ((0, padding), (0, 0), (0, 0), (0, 0)))
        value = value.reshape(count_t, slots, local_len, local_seqs, width)
        value = lax.all_to_all(value, "tensor", 0, 0, tiled=False)
        return value.transpose(1, 3, 0, 2, 4).reshape(rows, width)

    def give_back(value):
        value = value.reshape(slots, local_seqs, count_t, local_len, width)
        value = lax.all_to_all(value.transpose(2, 0, 3, 1, 4), "tensor", 0, 0, tiled=False)
        value = value.reshape(slots * count_t, local_len, local_seqs, width)[:micro]
        return features_out(value)

    packed = jnp.concatenate(
        [item[0].astype(F32).reshape(-1) for item in (norm_gains, vec_bias, b_qkv, b_up)]
    )
    every = lax.all_gather(packed, ("x", "core", "tensor"), axis=0, tiled=False)
    every = every.reshape(count_x, count_c, count_t, -1)
    sizes = [norm_gains.size, vec_bias.size, b_qkv.size, b_up.size]
    ends = [sum(sizes[: i + 1]) for i in range(len(sizes))]
    piece_gain, piece_shift, piece_bqkv, piece_bup = jnp.split(every, ends[:-1], axis=-1)

    def feature_vectors(piece, count):
        piece = piece.reshape(count_x, count_c, count_t, count, -1)
        return piece.transpose(3, 1, 0, 2, 4).reshape(count, width)

    def group_vectors(piece, shape):
        piece = piece.reshape(count_x, count_c, count_t, shape[1], shape[2])
        return piece.transpose(2, 3, 0, 1, 4).reshape(count_t, -1)

    gains = feature_vectors(piece_gain, norm_gains.shape[1])
    shifts = feature_vectors(piece_shift, vec_bias.shape[1])
    bias_qkv = group_vectors(piece_bqkv, b_qkv.shape)
    bias_up = group_vectors(piece_bup, b_up.shape)

    start_rows = collect(acts_in)

    def gather_rows(weight):
        stacked = gather_stack(gather_stack(gather_stack(weight, "tensor"), "x"), "core")
        shape = stacked.shape
        return jnp.moveaxis(stacked, 2, 0).reshape(count_t, -1, shape[-1])

    def gather_columns(weight):
        stacked = lax.all_gather(weight, "tensor", axis=0, tiled=True)
        stacked = gather_stack(gather_stack(stacked, "x"), "core")
        return stacked.reshape(count_c * count_x, -1, weight.shape[1])

    mat_qkv = gather_rows(w_qkv[0])
    mat_up = gather_rows(w_up[0])
    mat_out = gather_columns(w_out[0])
    mat_down = gather_columns(w_down[0])
    params = (gains, shifts, mat_qkv, bias_qkv, mat_out, mat_up, bias_up, mat_down)
    tables = rotation_tables(length, head_dim)

    inputs = start_rows
    for step in range(sections):
        result, stash = forward(inputs, params, tables, length, head_dim)
        if step < sections - 1:
            received = lax.ppermute(result, "section", [(i, i + 1) for i in range(sections - 1)])
            inputs = jnp.where(section_index == 0, start_rows, received)
    acts_local = give_back(result)

    end_rows = collect(cotangent)
    upstream = end_rows
    for step in range(sections):
        d_inputs, grads, small = backward(
            inputs, upstream, params, stash, tables, length, head_dim
        )
        if step < sections - 1:
            received = lax.ppermute(d_inputs, "section", [(i + 1, i) for i in range(sections - 1)])
            upstream = jnp.where(section_index == sections - 1, end_rows, received)
    grad_local = give_back(d_inputs)

    grad_qkv, grad_out, grad_up, grad_down = grads

    def share_rows(grad):
        grad = grad.reshape(count_t, count_c, count_x, -1, grad.shape[-1])
        grad = scatter_sum(jnp.moveaxis(grad, 1, 0), "core").astype(BF16)
        grad = scatter_sum(jnp.moveaxis(grad, 1, 0), "x")
        return lax.psum_scatter(
            grad.astype(BF16), "tensor", scatter_dimension=0, tiled=False
        ).astype(F32)

    def share_columns(grad):
        grad = grad.reshape(count_c, count_x, grad.shape[1], grad.shape[2])
        grad = scatter_sum(grad, "core").astype(BF16)
        grad = scatter_sum(grad, "x")
        return lax.psum_scatter(
            grad.astype(BF16), "tensor", scatter_dimension=0, tiled=True
        ).astype(F32)

    share_down = share_columns(grad_down)
    share_up = share_rows(grad_up)
    share_out = share_columns(grad_out)
    share_qkv = share_rows(grad_qkv)

    def feature_pieces(value):
        value = value.reshape(value.shape[0], count_c, count_x, count_t, -1)
        return value.transpose(2, 1, 3, 0, 4).reshape(count_x, count_c, count_t, -1)

    def group_pieces(value, shape):
        value = value.reshape(count_t, shape[1], count_x, count_c, shape[2])
        return value.transpose(2, 3, 0, 1, 4).reshape(count_x, count_c, count_t, -1)

    small_pieces = jnp.concatenate(
        [
            feature_pieces(small[0]),
            feature_pieces(small[1]),
            group_pieces(small[2], b_qkv.shape),
            group_pieces(small[3], b_up.shape),
        ],
        axis=-1,
    ).reshape(count_x * count_c * count_t, -1)
    share_small = lax.psum_scatter(
        small_pieces, ("x", "core", "tensor"), scatter_dimension=0, tiled=False
    )
    share_gain, share_shift, share_bqkv, share_bup = jnp.split(share_small, ends[:-1])
    return (
        acts_local[None],
        grad_local[None],
        share_gain.reshape(norm_gains.shape),
        share_shift.reshape(vec_bias.shape),
        share_qkv[None],
        share_bqkv.reshape(b_qkv.shape),
        share_out[None],
        share_up[None],
        share_bup.reshape(b_up.shape),
        share_down[None],
    )


def solution(mesh):
    sizes = mesh.shape
    cores = 2
    devices = mesh.devices.reshape(
        sizes["section"], sizes["dp"] // cores, cores, sizes["tensor"]
    )
    split = Mesh(devices, ("section", "x", "core", "tensor"))
    dp = ("x", "core")
    rows = P(None, "tensor", dp, None)
    vectors = P("section", None, ("x", "core", "tensor"))
    by_rows = P("section", dp, "tensor")
    by_columns = P("section", "tensor", dp)
    stacked = P("section", None, "tensor", dp, None)
    weights = (by_rows, by_columns, by_columns, by_rows, by_columns, by_columns)
    return jax.shard_map(
        local,
        mesh=split,
        in_specs=(rows, rows, vectors, vectors) + weights,
        out_specs=(stacked, stacked, vectors, vectors) + weights,
        check_vma=False,
    )
```

time: 2170 us -> 1340 us (0.62)
  waiting for transfers between devices: 1230 us -> 178 us
  matrix products: 471 us -> 241 us
  Pallas kernels: 0 us -> 203 us
  blocking collectives: 102 us -> 277 us
  local copies, waits for them, and re-layouts: 98.2 us -> 267 us
  other arithmetic: 220 us -> 111 us
    reduce_scatter x14 -> x4, waiting for transfers between devices: 760 us -> 0.01 us  [the longest x2 0.01 us: share_columns(): lax.psum_scatter(grad.astype(BF16), 'tensor', scatter_dimension=0, tiled=...]
    all_gather x13 -> x3, waiting for transfers between devices: 276 us -> 0.02 us  [the longest x2 0.02 us: gather_stack(): return lax.all_gather(value, axis, axis=0, tiled=False)]
    dot_general x130 -> x20, matrix products: 471 us -> 241 us  [product(): return jnp.einsum(equation, left, right, preferred_element_type=F32)]
    pallas_call x0 -> x4, Pallas kernels: none -> 203 us  [the longest x2 122 us: attention_back(): pl.pallas_call(attend_back_kernel, out_shape=jax.ShapeDtypeStruct(qkv.sha...]
    unnamed x0 -> x2, blocking collectives: none -> 185 us
    unnamed x35 -> x7, waiting for transfers between devices: 110 us -> 2.15 us
    reduce_sum x41 -> x7, other arithmetic: 93.7 us -> 15.5 us  [the longest x1 6.22 us: backward(): jnp.mean(d_scaled, axis=-1, keepdims=True)]
    ppermute x8 -> x18, waiting for transfers between devices: 85 us -> 160 us  [the longest x8 64.6 us: gather_stack(): other = lax.ppermute(value, axis, swap_pairs(axis))]
  transfers between devices with their start and end apart: 39 -> 29, of which waited for: 31 -> 7; matrix products, arithmetic and copies ran while one was open for 18% -> 34% of each run, Pallas kernels for 0% -> 3%
where the time goes in v1:
time: 1340 us; the launch traced here: 1330 us
  blocking collectives  277 us (21%)
  local copies, waits for them, and re-layouts  267 us (20%)
  matrix products  241 us (18%)
  Pallas kernels  203 us (15%)
  waiting for transfers between devices  178 us (13%)
  other arithmetic  111 us (8%)
  starting transfers between devices  33.9 us (3%)
  between operations  16.1 us (1%)
    dot_general x20, matrix products, product(): return jnp.einsum(equation, left, right, preferred_element_type=F32)  241 us
    unnamed x2, blocking collectives  185 us
    pallas_call x2, Pallas kernels, attention_back(): pl.pallas_call(attend_back_kernel, out_shape=jax.ShapeDtypeStruct(qkv.sha...  122 us
    all_gather x1, blocking collectives, gather_columns(): stacked = lax.all_gather(weight, 'tensor', axis=0, tiled=True)  91.9 us
    pallas_call x2, Pallas kernels, attention(): pl.pallas_call(attend_kernel, out_shape=jax.ShapeDtypeStruct((rows, group...  80.4 us
    ppermute x8, waiting for transfers between devices, gather_stack(): other = lax.ppermute(value, axis, swap_pairs(axis))  64.6 us
    transpose x2, local copies, waits for them, and re-layouts, gather_rows(): return jnp.moveaxis(stacked, 2, 0).reshape(count_t, -1, shape[-1])  37.7 us
    another operation x14, other arithmetic, gather_stack(): jnp.stack([jnp.where(first, value, other), jnp.where(first, other, value)])  33.9 us
  transfers between devices with their start and end apart: 29, of which 7 were waited for; matrix products, arithmetic and copies ran while one was open for 34% of the time, Pallas kernels for 3%

profile of v1, /device:TPU:0, one launch (start us, length us, event | category | flops | bytes accessed | tf_op | source)
XLA Modules:
  0.0 1326.6 jit_solution(9294415927751811200)
XLA Ops:
  16.1 6.3 all-to-all-start
  23.2 91.9 %all-gather.1 = bf16[1,1024,256]{2,1,0:T(8,128)(2,1)S(1)} all-gather(bf16[1,256,256]{2,1,0:T(8,128)(2,1)S(1)} %copy-done.31), channel_id=3, replica_groups=mesh['section'=2,'x'=2,'core'=2,'tensor'=4] {'tensor'}, dimensions={1}, use_global_device_ids=true | all-gather | bytes 655360 | tf_op jit(solution)/shard_map/all_gather | solution.py:346
  118.7 64.2 %all-reduce = f32[13312]{0:T(1024)S(1)} all-reduce(f32[13312]{0:T(1024)S(1)} %maximum_dynamic-update-slice_fusion), channel_id=2, replica_groups=mesh['section'=2,'x'=2,'core'=2,'tensor'=4] {'x','core','tensor'}, use_global_device_ids=true, to_apply=%add | all-reduce | flops 13312 | bytes 106496
  188.6 6.0 concatenate.34.ahead_ref
  194.6 5.9 concatenate.35.behind_ref
  200.9 4.5 reshape.340
  212.0 6.0 concatenate.33.keep_ref
  222.4 4.4 all-to-all-start.2
  242.1 25.7 %collective-permute-done.4 = bf16[4,256,1024]{2,1,0:T(8,128)(2,1)} collective-permute-done((bf16[4,256,1024]{2,1,0:T(8,128)(2,1)}, bf16[4,256,1024]{2,1,0:T(8,128)(2,1)}, u32[]{:S(2)}, u32[]{:S(2)}) %collective-permute-start.4) | collective-permute-done | bytes 2097184 | tf_op jit(solution)/shard_map/ppermute | solution.py:258
  273.4 38.9 %collective-permute-done.6 = bf16[4096,256]{1,0:T(8,128)(2,1)} collective-permute-done((bf16[4096,256]{1,0:T(8,128)(2,1)}, bf16[4096,256]{1,0:T(8,128)(2,1)}, u32[]{:S(2)}, u32[]{:S(2)}) %collective-permute-start.6) | collective-permute-done | bytes 2097184 | tf_op jit(solution)/shard_map/ppermute | solution.py:258
  320.5 16.4 %copy.228 = bf16[4,2,2,256,768]{3,2,1,4,0:T(2,128)(2,1)} copy(bf16[4,2,2,256,768]{4,3,0,2,1:T(8,128)(2,1)} %maximum_bitcast_fusion.1) | data formatting | bytes 12582912 | tf_op jit(solution)/shard_map/transpose | solution.py:343
  336.9 11.0 reshape.327
  347.9 11.1 fusion.9.qkv_ref
  359.0 40.3 %attend.2 = bf16[1024,1024]{1,0:T(8,128)(2,1)} custom-call(bf16[4,1024,768]{2,1,0:T(8,128)(2,1)} %fusion.9.qkv_ref, f32[1024,384]{1,0:T(8,128)} %concatenate.33.keep_ref, f32[1024,384]{1,0:T(8,128)} %concatenate.34.ahead_ref, f32[1024,384]{1,0:T(8,128)} %concatenate.35.behind_ref), custom_call_target="tpu_custom_call" | custom-call | flops 4294967296 | bytes 9437184 | tf_op jit(solution)/shard_map/attend/pallas_call | solution.py:146
  399.3 6.8 fusion.63
  406.2 5.1 select_bitcast_fusion.3
  411.3 7.5 maximum_bitcast_fusion
  418.8 21.4 %copy.236 = bf16[4,2,2,256,1024]{3,2,1,4,0:T(2,128)(2,1)} copy(bf16[4,2,2,256,1024]{4,3,0,2,1:T(8,128)(2,1)} %maximum_bitcast_fusion) | data formatting | bytes 16777216 | tf_op jit(solution)/shard_map/transpose | solution.py:343
  440.2 14.3 %reshape.333 = bf16[4,1024,1024]{1,2,0:T(8,128)(2,1)} reshape(bf16[4,2,2,256,1024]{3,2,1,4,0:T(2,128)(2,1)} %copy.236) | data formatting | bytes 16777216 | tf_op jit(solution)/shard_map/reshape | solution.py:343
  454.5 5.4 select_bitcast_fusion.1
  459.9 7.6 pad_maximum_fusion
  467.5 13.9 %multiply_convert_fusion.1 = bf16[1024,4,1024]{0,2,1:T(8,128)(2,1)} fusion(bf16[1024,1024,1]{1,0,2:T(8,128)(2,1)S(1)} %bitcast.313, bf16[4,1024,1024]{1,2,0:T(8,128)(2,1)} %reshape.333, f32[4,1024]{1,0:T(4,128)S(1)} %add.234), kind=kOutput, calls=%fused_computation.13 | convolution fusion | flops 8615100416 | bytes 18890752 | tf_op jit(solution)/shard_map/sk,tke->ste/dot_general | solution.py:184
  481.5 12.3 convolution_add_fusion.1
  504.2 4.5 reshape_reshape_transpose.3
  508.7 5.5 fusion.67.dctx_ref
  514.2 30.3 %collective-permute-done.8 = bf16[1024,1024]{0,1:T(8,128)(2,1)} collective-permute-done((bf16[1024,1024]{0,1:T(8,128)(2,1)}, bf16[1024,1024]{0,1:T(8,128)(2,1)}, u32[]{:S(2)}, u32[]{:S(2)}) %collective-permute-start.8) | collective-permute-done | bytes 2097184 | tf_op jit(solution)/shard_map/ppermute | solution.py:361
  546.3 21.8 %fusion.6 = (bf16[1024,4,1024]{0,2,1:T(8,128)(2,1)}, bf16[1024,4,1024]{0,2,1:T(8,128)(2,1)}) fusion(f32[4,1024]{1,0:T(4,128)S(1)} %add.234, bf16[4,1024,1024]{1,2,0:T(8,128)(2,1)} %reshape.333, bf16[1024,1024]{0,1:T(8,128)(2,1)S(1)} %get-tuple-element.22, f32[1024]{0:T(1024)S(1)} %add.231, f32[1024]{0:T(1024)S(1)} %mul.329, f32[1024]{0:T(1024)S(1)} %add_rsqrt_fusion, ...), kind=kOutput, calls=%fused_computation.9 | convolution fusion | flops 8646557696 | bytes 27295744 | tf_op jit(solution)/shard_map/sk,tke->ste/dot_general | solution.py:184
  568.1 12.1 fusion.10.qkv_ref
  580.2 15.0 %fusion = bf16[1024,4096]{0,1:T(8,128)(2,1)} fusion(bf16[1024,4096]{0,1:T(8,128)(2,1)S(1)} %bitcast.328, bf16[4,4096,256]{2,1,0:T(8,128)(2,1)} %bitcast.291, bf16[1024,4,256]{2,1,0:T(4,128)(2,1)S(1)} %copy-done.28), kind=kOutput, calls=%fused_computation.3 | convolution fusion | flops 8602517504 | bytes 27262976 | tf_op jit(solution)/shard_map/sbn,bkn->sk/dot_general | solution.py:184
  595.2 40.1 %attend.3 = bf16[1024,1024]{1,0:T(8,128)(2,1)} custom-call(bf16[4,1024,768]{2,1,0:T(8,128)(2,1)} %fusion.10.qkv_ref, f32[1024,384]{1,0:T(8,128)} %concatenate.33.keep_ref, f32[1024,384]{1,0:T(8,128)} %concatenate.34.ahead_ref, f32[1024,384]{1,0:T(8,128)} %concatenate.35.behind_ref), custom_call_target="tpu_custom_call" | custom-call | flops 4294967296 | bytes 9437184 | tf_op jit(solution)/shard_map/attend/pallas_call | solution.py:146
  635.4 61.2 %attend_back.2 = bf16[4,1024,768]{2,1,0:T(8,128)(2,1)} custom-call(bf16[4,1024,768]{2,1,0:T(8,128)(2,1)} %fusion.10.qkv_ref, bf16[1024,1024]{1,0:T(8,128)(2,1)} %fusion.67.dctx_ref, f32[1024,384]{1,0:T(8,128)} %concatenate.33.keep_ref, f32[1024,384]{1,0:T(8,128)} %concatenate.34.ahead_ref, f32[1024,384]{1,0:T(8,128)} %concatenate.35.behind_ref), custom_call_target="tpu_custom_call" | custom-call | flops 10737418240 | bytes 15728640 | tf_op jit(solution)/shard_map/attend_back/pallas_call | solution.py:165
  696.6 10.7 fusion.87
  707.3 15.2 %fusion.81 = (f32[1024]{0:T(1024)S(1)}, f32[1024]{0:T(1024)S(1)}, f32[1024,1024]{0,1:T(8,128)S(1)}) fusion(f32[1024]{0:T(1024)S(1)} %add_rsqrt_fusion, f32[1024]{0:T(1024)S(1)} %broadcast_multiply_fusion.4, bf16[1024,1024]{0,1:T(8,128)(2,1)S(1)} %get-tuple-element.22, f32[1024]{0:T(1024)S(1)} %mul.329, bf16[1024,4,1024]{0,2,1:T(8,128)(2,1)} %bitcast.329, ...), kind=kOutput, calls=%fused_computation.176 | convolution fusion | flops 8599369728 | bytes 27287552 | tf_op jit(solution)/shard_map/ste,tke->sk/dot_general | solution.py:184
  730.1 13.6 %convolution_add_fusion = f32[1024,4,256]{0,2,1:T(8,128)} fusion(f32[1024,4,256]{0,2,1:T(8,128)} %fusion.61, bf16[1024,4096,1]{0,1,2:T(8,128)(2,1)} %bitcast.325, bf16[4,4096,256]{2,1,0:T(8,128)(2,1)S(1)} %bitcast.295), kind=kOutput, calls=%fused_computation.101 | convolution fusion | flops 8590983168 | bytes 25165824 | tf_op jit(solution)/shard_map/sk,bkn->sbn/dot_general | solution.py:184
  743.7 31.6 %collective-permute-done.9 = bf16[1024,1024]{0,1:T(8,128)(2,1)} collective-permute-done((bf16[1024,1024]{0,1:T(8,128)(2,1)S(1)}, bf16[1024,1024]{0,1:T(8,128)(2,1)}, u32[]{:S(2)}, u32[]{:S(2)}) %collective-permute-start.9) | collective-permute-done | bytes 2097184 | tf_op jit(solution)/shard_map/ppermute | solution.py:372
  781.9 15.0 %convert_reduce_fusion = (f32[4096]{0:T(1024)}, bf16[1024,4096]{0,1:T(8,128)(2,1)}) fusion(bf16[1024,4096]{0,1:T(8,128)(2,1)} %bitcast.327, bf16[4,4096,256]{2,1,0:T(8,128)(2,1)S(1)} %bitcast.296, bf16[1024,4,256]{0,2,1:T(8,128)(2,1)S(1)} %bitcast.301), kind=kOutput, calls=%fused_computation.10 | convolution fusion | flops 8610902016 | bytes 27279360 | tf_op jit(solution)/shard_map/sbn,bkn->sk/dot_general | solution.py:184
  796.9 5.9 fusion.59
  802.8 61.0 %attend_back.3 = bf16[4,1024,768]{2,1,0:T(8,128)(2,1)} custom-call(bf16[4,1024,768]{2,1,0:T(8,128)(2,1)} %fusion.10.qkv_ref, bf16[1024,1024]{1,0:T(8,128)(2,1)} %bitcast_convert_fusion.dctx_ref, f32[1024,384]{1,0:T(8,128)} %concatenate.33.keep_ref, f32[1024,384]{1,0:T(8,128)} %concatenate.34.ahead_ref, f32[1024,384]{1,0:T(8,128)} %concatenate.35.behind_ref), custom_call_target="tpu_custom_call" | custom-call | flops 10737418240 | bytes 15728640 | tf_op jit(solution)/shard_map/attend_back/pallas_call | solution.py:165
  863.8 13.4 %convolution_bitcast_fusion = f32[4,1024,768]{1,2,0:T(8,128)} fusion(bf16[4,1024,768]{2,1,0:T(8,128)(2,1)} %attend_back.3, bf16[1024,1024]{0,1:T(8,128)(2,1)S(1)} %get-tuple-element.22, f32[1024]{0:T(1024)S(1)} %copy-done.39, f32[1024]{0:T(1024)S(1)} %copy-done.33, f32[1024]{0:T(1024)S(1)} %add_rsqrt_fusion, f32[1024]{0:T(1024)S(1)} %broadcast_multiply_fusion.4), kind=kOutput, calls=%fused_computation.50 | convolution fusion | flops 6448742400 | bytes 20987904 | tf_op jit(solution)/shard_map/sk,tse->tke/dot_general | solution.py:184
  877.2 16.9 %reshape.348 = f32[4,2,2,256,768]{3,2,1,4,0:T(2,128)} reshape(f32[4,1024,768]{1,2,0:T(8,128)} %convolution_bitcast_fusion) | data formatting | bytes 25165824 | tf_op jit(solution)/shard_map/reshape | solution.py:379
  894.1 6.6 constant_dynamic-slice_fusion.6
  900.7 8.6 copy.328
  912.9 11.9 fusion.73
  924.9 18.0 %fusion.86 = (f32[1024]{0:T(1024)S(1)}, f32[1024,1024]{1,0:T(8,128)}) fusion(bf16[4,1024,768]{2,1,0:T(8,128)(2,1)} %attend_back.3, bf16[4,1024,768]{1,2,0:T(8,128)(2,1)} %reshape.327), kind=kOutput, calls=%fused_computation.181 | convolution fusion | flops 6443498496 | bytes 16781312 | tf_op jit(solution)/shard_map/tse,tke->sk/dot_general | solution.py:184
  945.5 7.5 constant_dynamic-slice_fusion.7
  953.0 10.2 copy.277
  971.8 4.5 fusion.11
  980.6 14.6 %fusion.88 = f32[4,256,4096]{2,1,0:T(8,128)} fusion(bf16[1024,4,256]{0,2,1:T(8,128)(2,1)S(1)} %bitcast.303, bf16[1024,4096,1]{0,1,2:T(8,128)(2,1)} %bitcast.326), kind=kOutput, calls=%fused_computation.183 | convolution fusion | flops 8589934592 | bytes 27262976 | tf_op jit(solution)/shard_map/sk,sbn->bkn/dot_general | solution.py:184
  996.3 6.2 constant_dynamic-slice_fusion
  1002.4 6.3 copy.331
  1008.8 6.4 fusion.8
  1022.8 15.7 %fusion.85 = (f32[1024]{0:T(1024)S(1)}, f32[1024,1024]{1,0:T(8,128)}) fusion(bf16[1024,4,1024]{0,2,1:T(8,128)(2,1)} %bitcast.324, bf16[4,1024,1024]{1,2,0:T(8,128)(2,1)} %reshape.333), kind=kOutput, calls=%fused_computation.180 | convolution fusion | flops 8590982144 | bytes 20975616 | tf_op jit(solution)/shard_map/ste,tke->sk/dot_general | solution.py:184
  1038.5 5.4 copy.260
  1043.8 5.4 copy.266
  1049.2 7.7 constant_dynamic-slice_fusion.1
  1056.9 9.0 copy.285
  1065.9 6.2 fusion.80
  1076.0 6.2 fusion.7
  1099.5 32.8 %collective-permute-done.17 = bf16[4096,256]{1,0:T(8,128)(2,1)} collective-permute-done((bf16[4096,256]{1,0:T(8,128)(2,1)}, bf16[4096,256]{1,0:T(8,128)(2,1)}, u32[]{:S(2)}, u32[]{:S(2)}) %collective-permute-start.17) | collective-permute-done | bytes 2097184 | tf_op jit(solution)/shard_map/ppermute | solution.py:268
  1136.4 4.8 transpose_reshape.7
  1144.4 16.1 %all-to-all-done.1 = bf16[4,1,256,1,1024]{2,4,3,1,0:T(8,128)(2,1)S(1)} async-done(((bf16[4,1,256,1,1024]{2,4,3,1,0:T(8,128)(2,1)}), bf16[4,1,256,1,1024]{2,4,3,1,0:T(8,128)(2,1)S(1)}, u32[]{:S(2)}, u32[]{:S(2)}) %all-to-all-start.1) | async-done | bytes 2097184 | tf_op jit(solution)/shard_map/all_to_all | solution.py:312
  1160.4 4.5 all-to-all-start.3
  1169.7 121.2 %all-reduce.1 = f32[16,832]{1,0:T(8,128)S(1)} all-reduce(f32[16,832]{1,0:T(8,128)S(1)} %pad_maximum_fusion.6), channel_id=5, replica_groups=mesh['section'=2,'x'=2,'core'=2,'tensor'=4] {'x','core','tensor'}, use_global_device_ids=true, to_apply=%region_15.16.clone | all-reduce | flops 13312 | bytes 106496
  1305.6 4.8 copy.268
  (284 shorter events, 169.0 us)
Async XLA Ops:
  7.2 178.0 %all-gather.7.cloned.1.call-start = ((), (), s32[]{:S(2)}) async-start(), calls=%async_computation.8 | async-start | bytes 1966080 | tf_op jit(solution)/shard_map/all_gather | solution.py:261
  7.9 210.0 %all-gather.9.cloned.1.call-start = ((), (), s32[]{:S(2)}) async-start(), calls=%async_computation.9 | async-start | bytes 2621440 | tf_op jit(solution)/shard_map/all_gather | solution.py:261
  12.0 11.2 copy-start.31
  12.0 104.9 %copy-start.43 = (bf16[1,8,32]{2,1,0:T(8,128)(2,1)S(1)}, bf16[1,8,32]{2,1,0:T(8,128)(2,1)}, u32[]{:S(2)}) copy-start(bf16[1,8,32]{2,1,0:T(8,128)(2,1)} %param.18) | copy-start | bytes 1540
  12.0 105.0 %copy-start.45 = (bf16[1,4,48]{2,1,0:T(4,128)(2,1)S(1)}, bf16[1,4,48]{2,1,0:T(4,128)(2,1)}, u32[]{:S(2)}) copy-start(bf16[1,4,48]{2,1,0:T(4,128)(2,1)} %param.15) | copy-start | bytes 1156
  12.0 105.1 %copy-start.44 = (f32[1,4,64]{2,1,0:T(4,128)S(1)}, f32[1,4,64]{2,1,0:T(4,128)}, u32[]{:S(2)}) copy-start(f32[1,4,64]{2,1,0:T(4,128)} %param.13) | copy-start | bytes 3076
  12.0 105.1 %copy-start.46 = (f32[1,2,64]{2,1,0:T(2,128)S(1)}, f32[1,2,64]{2,1,0:T(2,128)}, u32[]{:S(2)}) copy-start(f32[1,2,64]{2,1,0:T(2,128)} %param.12) | copy-start | bytes 1540
  12.0 105.2 %copy-start.42 = (u32[32]{0:T(128)S(1)}, u32[32]{0:T(128)}, u32[]{:S(2)}) copy-start(u32[32]{0:T(128)} %constant.112) | copy-start | bytes 388
  16.1 206.3 %all-to-all-start = ((bf16[4,1,256,1,1024]{2,4,3,1,0:T(8,128)(2,1)}), bf16[4,1,256,1,1024]{2,4,3,1,0:T(8,128)(2,1)}, u32[]{:S(2)}, u32[]{:S(2)}) async-start(bf16[4,1,256,1,1024]{2,4,3,1,0:T(8,128)(2,1)} %bitcast.1), calls=%async_computation | async-start | bytes 4194304 | tf_op jit(solution)/shard_map/all_to_all | solution.py:307
  22.5 209.9 %all-gather.11.cloned.1.call-start = ((), (), s32[]{:S(2)}) async-start(), calls=%async_computation.14 | async-start | bytes 2621440 | tf_op jit(solution)/shard_map/all_gather | solution.py:346
  115.1 68.0 %collective-permute-start.2 = (bf16[1024,256]{1,0:T(8,128)(2,1)S(1)}, bf16[1024,256]{1,0:T(8,128)(2,1)S(1)}, u32[]{:S(2)}, u32[]{:S(2)}) collective-permute-start(bf16[1024,256]{1,0:T(8,128)(2,1)S(1)} %bitcast.308), channel_id=1, source_target_pairs={{0,8},{8,0},{1,9},{9,1},{2,10},{10,2},{3,11},{11,3},{4,12},{12,4},... | collective-permute-start | bytes 1572872 | tf_op jit(solution)/shard_map/ppermute | solution.py:258
  185.0 34.5 %collective-permute-start.3 = (bf16[2,1024,256]{2,1,0:T(8,128)(2,1)}, bf16[2,1024,256]{2,1,0:T(8,128)(2,1)}, u32[]{:S(2)}, u32[]{:S(2)}) collective-permute-start(bf16[2,1024,256]{2,1,0:T(8,128)(2,1)} %pad_maximum_fusion.5), channel_id=1, source_target_pairs={{0,4},{4,0},{1,5},{5,1},{2,6},{6,2},{3,7},{7,3},{8,12},{12,8},{9,1... | collective-permute-start | bytes 3145736 | tf_op jit(solution)/shard_map/ppermute | solution.py:258
  185.2 51.0 %collective-permute-start = (bf16[4,256,768]{2,1,0:T(8,128)(2,1)}, bf16[4,256,768]{2,1,0:T(8,128)(2,1)}, u32[]{:S(2)}, u32[]{:S(2)}) collective-permute-start(bf16[4,256,768]{2,1,0:T(8,128)(2,1)} %all-gather.7.cloned.1.call-done), channel_id=1, source_target_pairs={{0,8},{8,0},{1,9},{9,1},{2,10},{10,2},{3,11},{11,3},{4,12},{12,4},... | collective-permute-start | bytes 4718600 | tf_op jit(solution)/shard_map/ppermute | solution.py:258
  186.1 360.1 %copy-start.36 = (f32[1024]{0:T(1024)}, f32[1024]{0:T(1024)S(1)}, u32[]{:S(2)}) copy-start(f32[1024]{0:T(1024)S(1)} %add.231) | copy-start | bytes 12292
  186.4 53.0 %copy-start.38 = (f32[1024]{0:T(1024)}, f32[1024]{0:T(1024)S(1)}, u32[]{:S(2)}) copy-start(f32[1024]{0:T(1024)S(1)} %add.223) | copy-start | bytes 12292
  186.5 53.0 %copy-start.32 = (f32[1024]{0:T(1024)}, f32[1024]{0:T(1024)S(1)}, u32[]{:S(2)}) copy-start(f32[1024]{0:T(1024)S(1)} %mul.322) | copy-start | bytes 12292
  200.9 292.9 %copy-start.34 = (f32[1024]{0:T(1024)}, f32[1024]{0:T(1024)S(1)}, u32[]{:S(2)}) copy-start(f32[1024]{0:T(1024)S(1)} %add.241) | copy-start | bytes 12292
  211.9 7.6 copy-start.20
  212.0 7.6 copy-start.22
  217.9 49.9 %collective-permute-start.4 = (bf16[4,256,1024]{2,1,0:T(8,128)(2,1)}, bf16[4,256,1024]{2,1,0:T(8,128)(2,1)}, u32[]{:S(2)}, u32[]{:S(2)}) collective-permute-start(bf16[4,256,1024]{2,1,0:T(8,128)(2,1)} %all-gather.9.cloned.1.call-done), channel_id=1, source_target_pairs={{0,8},{8,0},{1,9},{9,1},{2,10},{10,2},{3,11},{11,3},{4,12},{12,4},... | collective-permute-start | bytes 6291464 | tf_op jit(solution)/shard_map/ppermute | solution.py:258
  222.4 277.6 %all-to-all-start.2 = ((bf16[4,1,256,1,1024]{4,2,3,1,0:T(8,128)(2,1)}), bf16[4,1,256,1,1024]{4,2,3,1,0:T(8,128)(2,1)}, u32[]{:S(2)}, u32[]{:S(2)}) async-start(bf16[4,1,256,1,1024]{4,2,3,1,0:T(8,128)(2,1)} %reshape_reshape.14), calls=%async_computation.2 | async-start | bytes 4194304 | tf_op jit(solution)/shard_map/all_to_all | solution.py:307
  226.8 1068.8 %reduce-scatter.7.cloned.1.call-start = ((), (), s32[]{:S(2)}) async-start(), calls=%async_computation.11 | async-start | bytes 655360 | tf_op jit(solution)/shard_map/reduce_scatter | solution.py:390
  232.4 79.9 %collective-permute-start.6 = (bf16[4096,256]{1,0:T(8,128)(2,1)}, bf16[4096,256]{1,0:T(8,128)(2,1)}, u32[]{:S(2)}, u32[]{:S(2)}) collective-permute-start(bf16[4096,256]{1,0:T(8,128)(2,1)} %bitcast.315), channel_id=1, source_target_pairs={{0,8},{8,0},{1,9},{9,1},{2,10},{10,2},{3,11},{11,3},{4,12},{12,4},... | collective-permute-start | bytes 6291464 | tf_op jit(solution)/shard_map/ppermute | solution.py:258
  238.6 29.2 %copy-start.29 = (bf16[4,256,1024]{2,1,0:T(8,128)(2,1)S(1)}, bf16[4,256,1024]{2,1,0:T(8,128)(2,1)}, u32[]{:S(2)}) copy-start(bf16[4,256,1024]{2,1,0:T(8,128)(2,1)} %all-gather.9.cloned.1.call-done) | copy-start | bytes 6291460
  238.6 78.2 %collective-permute-start.1 = (bf16[2,4,256,768]{3,2,1,0:T(8,128)(2,1)S(1)}, bf16[2,4,256,768]{3,2,1,0:T(8,128)(2,1)S(1)}, u32[]{:S(2)}, u32[]{:S(2)}) collective-permute-start(bf16[2,4,256,768]{3,2,1,0:T(8,128)(2,1)S(1)} %pad_maximum_fusion.3), channel_id=1, source_target_pairs={{0,4},{4,0},{1,5},{5,1},{2,6},{6,2},{3,7},{7,3},{8,12},{12,8},{9,1... | collective-permute-start | bytes 9437192 | tf_op jit(solution)/shard_map/ppermute | solution.py:258
  269.9 42.3 %copy-start.30 = (bf16[1,4096,256]{2,1,0:T(8,128)(2,1)S(1)}, bf16[1,4096,256]{2,1,0:T(8,128)(2,1)}, u32[]{:S(2)}) copy-start(bf16[1,4096,256]{2,1,0:T(8,128)(2,1)} %all-gather.11.cloned.1.call-done) | copy-start | bytes 6291460
  273.4 132.8 %collective-permute-start.5 = (bf16[2,4,256,1024]{3,2,1,0:T(8,128)(2,1)}, bf16[2,4,256,1024]{3,2,1,0:T(8,128)(2,1)}, u32[]{:S(2)}, u32[]{:S(2)}) collective-permute-start(bf16[2,4,256,1024]{3,2,1,0:T(8,128)(2,1)} %pad_maximum_fusion.1), channel_id=1, source_target_pairs={{0,4},{4,0},{1,5},{5,1},{2,6},{6,2},{3,7},{7,3},{8,12},{12,8},{9,1... | collective-permute-start | bytes 12582920 | tf_op jit(solution)/shard_map/ppermute | solution.py:258
  316.8 137.7 %collective-permute-start.7 = (bf16[2,4096,256]{2,1,0:T(8,128)(2,1)}, bf16[2,4096,256]{2,1,0:T(8,128)(2,1)}, u32[]{:S(2)}, u32[]{:S(2)}) collective-permute-start(bf16[2,4096,256]{2,1,0:T(8,128)(2,1)} %pad_maximum_fusion.2), channel_id=1, source_target_pairs={{0,4},{4,0},{1,5},{5,1},{2,6},{6,2},{3,7},{7,3},{8,12},{12,8},{9,1... | collective-permute-start | bytes 12582920 | tf_op jit(solution)/shard_map/ppermute | solution.py:258
  399.3 6.8 copy-start.5
  459.9 7.6 copy-start.27
  467.5 13.9 %copy-start.15 = (bf16[2,2,4096,256]{3,2,1,0:T(8,128)(2,1)S(1)}, bf16[2,2,4096,256]{3,2,1,0:T(8,128)(2,1)}, u32[]{:S(2)}) copy-start(bf16[2,2,4096,256]{3,2,1,0:T(8,128)(2,1)} %pad_maximum_fusion) | copy-start | bytes 25165828
  481.5 12.3 copy-start.6
  495.6 49.0 %collective-permute-start.8 = (bf16[1024,1024]{0,1:T(8,128)(2,1)}, bf16[1024,1024]{0,1:T(8,128)(2,1)}, u32[]{:S(2)}, u32[]{:S(2)}) collective-permute-start(bf16[1024,1024]{0,1:T(8,128)(2,1)} %fusion.54), channel_id=1, source_target_pairs={{0,16},{1,17},{2,18},{3,19},{4,20},{5,21},{6,22},{7,23},{8,24},{9,... | collective-permute-start | bytes 6291464 | tf_op jit(solution)/shard_map/ppermute | solution.py:361
  500.0 8.6 copy-start.24
  508.7 35.9 %copy-start.7 = (bf16[128,8,4,256]{3,1,2,0:T(8,128)(2,1)S(1)}, bf16[128,8,4,256]{3,1,2,0:T(8,128)(2,1)}, u32[]{:S(2)}) copy-start(bf16[128,8,4,256]{3,1,2,0:T(8,128)(2,1)} %copy.332) | copy-start | bytes 6291460
  546.2 21.9 %copy-start.33 = (f32[1024]{0:T(1024)S(1)}, f32[1024]{0:T(1024)}, u32[]{:S(2)}) copy-start(f32[1024]{0:T(1024)} %copy-done.32) | copy-start | bytes 12292
  546.2 21.9 %copy-start.39 = (f32[1024]{0:T(1024)S(1)}, f32[1024]{0:T(1024)}, u32[]{:S(2)}) copy-start(f32[1024]{0:T(1024)} %copy-done.38) | copy-start | bytes 12292
  568.1 12.1 copy-start.28
  568.1 12.1 copy-start.47
  707.3 15.2 %copy-start = (bf16[1024,1024]{0,1:T(8,128)(2,1)S(1)}, bf16[1024,1024]{0,1:T(8,128)(2,1)}, u32[]{:S(2)}) copy-start(bf16[1024,1024]{0,1:T(8,128)(2,1)} %copy.315) | copy-start | bytes 6291460
  722.5 7.5 slice-start
  724.1 51.2 %collective-permute-start.9 = (bf16[1024,1024]{0,1:T(8,128)(2,1)S(1)}, bf16[1024,1024]{0,1:T(8,128)(2,1)}, u32[]{:S(2)}, u32[]{:S(2)}) collective-permute-start(bf16[1024,1024]{0,1:T(8,128)(2,1)S(1)} %fusion.38), channel_id=1, source_target_pairs={{16,0},{17,1},{18,2},{19,3},{20,4},{21,5},{22,6},{23,7},{24,8},{25... | collective-permute-start | bytes 6291464 | tf_op jit(solution)/shard_map/ppermute | solution.py:372
  743.7 34.5 %copy-start.26 = (bf16[2,2,1024,256]{3,2,1,0:T(8,128)(2,1)S(1)}, bf16[2,2,1024,256]{3,2,1,0:T(8,128)(2,1)}, u32[]{:S(2)}) copy-start(bf16[2,2,1024,256]{3,2,1,0:T(8,128)(2,1)} %pad_maximum_fusion.4) | copy-start | bytes 6291460
  778.1 18.7 %copy-start.16 = (bf16[1024,1024]{0,1:T(8,128)(2,1)}, bf16[1024,1024]{0,1:T(8,128)(2,1)S(1)}, u32[]{:S(2)}) copy-start(bf16[1024,1024]{0,1:T(8,128)(2,1)S(1)} %get-tuple-element.19) | copy-start | bytes 6291460
  900.7 12.2 copy-start.37
  909.3 62.4 %collective-permute-start.10 = (bf16[4,2,256,768]{3,2,0,1:T(8,128)(2,1)}, bf16[4,2,256,768]{3,2,0,1:T(8,128)(2,1)}, u32[]{:S(2)}, u32[]{:S(2)}) collective-permute-start(bf16[4,2,256,768]{3,2,0,1:T(8,128)(2,1)} %bitcast.305), channel_id=1, source_target_pairs={{0,4},{4,0},{1,5},{5,1},{2,6},{6,2},{3,7},{7,3},{8,12},{12,8},{9,1... | collective-permute-start | bytes 9437192 | tf_op jit(solution)/shard_map/ppermute | solution.py:268
  912.4 56.9 %collective-permute-start.12 = (bf16[2,1024,256]{2,1,0:T(8,128)(2,1)}, bf16[2,1024,256]{2,1,0:T(8,128)(2,1)S(1)}, u32[]{:S(2)}, u32[]{:S(2)}) collective-permute-start(bf16[2,1024,256]{2,1,0:T(8,128)(2,1)} %bitcast.316), channel_id=1, source_target_pairs={{0,4},{4,0},{1,5},{5,1},{2,6},{6,2},{3,7},{7,3},{8,12},{12,8},{9,1... | collective-permute-start | bytes 3145736 | tf_op jit(solution)/shard_map/ppermute | solution.py:268
  924.8 18.0 %copy-start.14 = (f32[4,1024,1024]{1,2,0:T(8,128)}, f32[4,1024,1024]{1,2,0:T(8,128)S(1)}, u32[]{:S(2)}) copy-start(f32[4,1024,1024]{1,2,0:T(8,128)S(1)} %fusion.73) | copy-start | bytes 50331652
  945.5 63.3 %collective-permute-start.14 = (bf16[4,2,256,1024]{3,2,0,1:T(8,128)(2,1)}, bf16[4,2,256,1024]{3,2,0,1:T(8,128)(2,1)}, u32[]{:S(2)}, u32[]{:S(2)}) collective-permute-start(bf16[4,2,256,1024]{3,2,0,1:T(8,128)(2,1)} %fusion.49), channel_id=1, source_target_pairs={{0,4},{4,0},{1,5},{5,1},{2,6},{6,2},{3,7},{7,3},{8,12},{12,8},{9,1... | collective-permute-start | bytes 12582920 | tf_op jit(solution)/shard_map/ppermute | solution.py:268
  971.2 9.5 copy-start.17
  971.2 24.1 %collective-permute-start.13 = (bf16[1024,256]{1,0:T(8,128)(2,1)S(1)}, bf16[1024,256]{1,0:T(8,128)(2,1)S(1)}, u32[]{:S(2)}, u32[]{:S(2)}) collective-permute-start(bf16[1024,256]{1,0:T(8,128)(2,1)S(1)} %dynamic-slice_bitcast_fusion.3), channel_id=1, source_target_pairs={{0,8},{8,0},{1,9},{9,1},{2,10},{10,2},{3,11},{11,3},{4,12},{12,4},... | collective-permute-start | bytes 1572872 | tf_op jit(solution)/shard_map/ppermute | solution.py:268
  979.2 40.3 %collective-permute-start.11 = (bf16[4,256,768]{2,1,0:T(8,128)(2,1)}, bf16[4,256,768]{2,1,0:T(8,128)(2,1)}, u32[]{:S(2)}, u32[]{:S(2)}) collective-permute-start(bf16[4,256,768]{2,1,0:T(8,128)(2,1)} %dynamic-slice_bitcast_fusion.2), channel_id=1, source_target_pairs={{0,8},{8,0},{1,9},{9,1},{2,10},{10,2},{3,11},{11,3},{4,12},{12,4},... | collective-permute-start | bytes 4718600 | tf_op jit(solution)/shard_map/ppermute | solution.py:268
  996.2 317.0 %reduce-scatter.5.cloned.1.call-start = ((), (), s32[]{:S(2)}) async-start(), calls=%async_computation.10 | async-start | bytes 1966080 | tf_op jit(solution)/shard_map/reduce_scatter | solution.py:382
  1008.8 67.2 %collective-permute-start.16 = (bf16[2,4096,256]{2,1,0:T(8,128)(2,1)}, bf16[2,4096,256]{2,1,0:T(8,128)(2,1)}, u32[]{:S(2)}, u32[]{:S(2)}) collective-permute-start(bf16[2,4096,256]{2,1,0:T(8,128)(2,1)} %bitcast.304), channel_id=1, source_target_pairs={{0,4},{4,0},{1,5},{5,1},{2,6},{6,2},{3,7},{7,3},{8,12},{12,8},{9,1... | collective-permute-start | bytes 12582920 | tf_op jit(solution)/shard_map/ppermute | solution.py:268
  1018.6 53.4 %collective-permute-start.15 = (bf16[4,256,1024]{2,1,0:T(8,128)(2,1)}, bf16[4,256,1024]{2,1,0:T(8,128)(2,1)}, u32[]{:S(2)}, u32[]{:S(2)}) collective-permute-start(bf16[4,256,1024]{2,1,0:T(8,128)(2,1)} %dynamic-slice_bitcast_fusion.1), channel_id=1, source_target_pairs={{0,8},{8,0},{1,9},{9,1},{2,10},{10,2},{3,11},{11,3},{4,12},{12,4},... | collective-permute-start | bytes 6291464 | tf_op jit(solution)/shard_map/ppermute | solution.py:268
  1022.7 292.4 %reduce-scatter.9.cloned.1.call-start = ((), (), s32[]{:S(2)}) async-start(), calls=%async_computation.12 | async-start | bytes 2621440 | tf_op jit(solution)/shard_map/reduce_scatter | solution.py:382
  1076.0 8.6 copy-start.18
  1076.0 8.6 copy-start.23
  1082.2 8.6 copy-start.11
  1083.8 48.5 %collective-permute-start.17 = (bf16[4096,256]{1,0:T(8,128)(2,1)}, bf16[4096,256]{1,0:T(8,128)(2,1)}, u32[]{:S(2)}, u32[]{:S(2)}) collective-permute-start(bf16[4096,256]{1,0:T(8,128)(2,1)} %dynamic-slice_bitcast_fusion), channel_id=1, source_target_pairs={{0,8},{8,0},{1,9},{9,1},{2,10},{10,2},{3,11},{11,3},{4,12},{12,4},... | collective-permute-start | bytes 6291464 | tf_op jit(solution)/shard_map/ppermute | solution.py:268
  1095.8 64.6 %all-to-all-start.1 = ((bf16[4,1,256,1,1024]{2,4,3,1,0:T(8,128)(2,1)}), bf16[4,1,256,1,1024]{2,4,3,1,0:T(8,128)(2,1)S(1)}, u32[]{:S(2)}, u32[]{:S(2)}) async-start(bf16[4,1,256,1,1024]{2,4,3,1,0:T(8,128)(2,1)} %copy.245), calls=%async_computation.1 | async-start | bytes 4194304 | tf_op jit(solution)/shard_map/all_to_all | solution.py:312
  1099.4 217.8 %reduce-scatter.11.cloned.1.call-start = ((), (), s32[]{:S(2)}) async-start(), calls=%async_computation.13 | async-start | bytes 2621440 | tf_op jit(solution)/shard_map/reduce_scatter | solution.py:390
  1141.1 23.8 %copy-start.40 = (f32[4096]{0:T(1024)S(1)}, f32[4096]{0:T(1024)}, u32[]{:S(2)}) copy-start(f32[4096]{0:T(1024)} %get-tuple-element.58) | copy-start | bytes 49156
  1160.4 145.2 %all-to-all-start.3 = ((bf16[4,1,256,1,1024]{2,4,3,1,0:T(8,128)(2,1)}), bf16[4,1,256,1,1024]{2,4,3,1,0:T(8,128)(2,1)}, u32[]{:S(2)}, u32[]{:S(2)}) async-start(bf16[4,1,256,1,1024]{2,4,3,1,0:T(8,128)(2,1)} %copy.267), calls=%async_computation.3 | async-start | bytes 4194304 | tf_op jit(solution)/shard_map/all_to_all | solution.py:312
  (16 other events, 56.3 us)
Sparse Core Ops, SparseCore 0:
  9.6 62.8 all-gather.6
  74.0 63.1 all-gather.8
  138.8 45.6 all-gather.10
  996.3 18.2 reduce-scatter.6
  1022.9 32.0 reduce-scatter.4
  1076.1 55.9 reduce-scatter.8
  1136.5 82.2 reduce-scatter.10
